TPU v7x, 256 devices: a whole 4x4x8 slice. The times are simulated.
256 devices in a mesh: px: 4 (over z_lo), py: 8 (over y, core), ch: 8 (over z_hi, x).
Axes of the slice: x: 4, y: 4, z: 8 (z_hi: 2, z_lo: 4; z = z_hi * 4 + z_lo), core: 2. Of those that a mesh axis runs over, the one named last changes fastest.
Arguments:
- features: bfloat16 [128, 12, 8, 4, 512], P('ch', None, 'py', 'px'), may hold values from -6 to 6
- cotangent: bfloat16 [128, 12, 8, 4, 512], P('ch', None, 'py', 'px'), may hold values from -6 to 6
- weight: bfloat16 [3, 3, 128, 128], replicated, may hold values from -0.1875 to 0.1875
- edge_table: int32 [12, 4, 3], replicated, may hold values from 0 to 11, as said below
- corner_table: int32 [12, 4, 2], replicated, may hold values from 0 to 11, as said below
Outputs:
- activation: bfloat16 [128, 12, 8, 4, 512], P('ch', None, 'py', 'px')
- input_grad: bfloat16 [128, 12, 8, 4, 512], P('ch', None, 'py', 'px')
Inputs may be any that keep to these rules, and one draw needn't show every extreme that they name: edge_table[f, e] = (g, s, r): beyond edge e of face f lie the pixels of side s of face g, in reverse order if r = 1; every side of every face is named exactly once, and if (f, e) names (g, s) then (g, s) names (f, e) with the same r. corner_table[f, c] = (h, q): corner c of face f takes corner pixel q of face h; in each corner column every face appears once, and each q appears 12 times.
All inputs are finite; a program needn't handle non-finite values.
Results may differ from a plain program's by a relative error of at most 0.0049.
Values may be sent and summed in bfloat16 or wider, within the bound.
A program may use at most 192 MiB of HBM per device.

v0:
```python
import jax
import jax.numpy as jnp
from jax import lax
from jax.sharding import PartitionSpec as P

RB = 32


def with_halo(array, sides, width):
    for axis, dim in sides:
        size, length = (lax.axis_size(axis), array.shape[dim])
        up = [(i, (i + 1) % size) for i in range(size - 1)]
        down = [(j, i) for i, j in up]
        last = lax.slice_in_dim(array, length - width, length, axis=dim)
        leading = lax.slice_in_dim(array, 0, width, axis=dim)
        before = lax.ppermute(last, axis, up)
        after = lax.ppermute(leading, axis, down)
        array = jnp.concatenate([before, array, after], axis=dim)
    return array


def edge_strips(lines, edge_table, corner_table):
    chan_count = lines.shape[0]
    face_count = lines.shape[1]
    side_len = lines.shape[3]
    flat_lines = lines.reshape(chan_count, face_count * 4, side_len)
    pixels = jnp.stack(
        [lines[:, :, 0, 0], lines[:, :, 0, -1], lines[:, :, 1, 0], lines[:, :, 1, -1]], axis=2
    ).reshape(chan_count, face_count * 4)
    corner_index = corner_table[:, :, 0] * 4 + corner_table[:, :, 1]
    corner_vals = jnp.take(pixels, corner_index, axis=1)
    strips = []
    for edge_num, start_corner, end_corner in ((0, 0, 1), (1, 2, 3), (2, 0, 2), (3, 1, 3)):
        source_row = edge_table[:, edge_num, 0] * 4 + edge_table[:, edge_num, 1]
        strip_line = jnp.take(flat_lines, source_row, axis=1)
        flipped = (edge_table[:, edge_num, 2] == 1)[None, :, None]
        strip_line = jnp.where(flipped, strip_line[:, :, ::-1], strip_line)
        strips.append(
            jnp.concatenate(
                [
                    corner_vals[:, :, start_corner : start_corner + 1],
                    strip_line,
                    corner_vals[:, :, end_corner : end_corner + 1],
                ],
                axis=2,
            )
        )
    return strips


def face_lines_of(field, row_pos, col_pos, px_count, py_count):
    chan_block = field.shape[0]
    face_count = field.shape[1]
    col_len = field.shape[2]
    row_len = field.shape[3]
    side_len = row_len * px_count
    blank = jnp.zeros((chan_block, face_count, side_len), jnp.float32)

    def placed(values, offset, active):
        return jnp.where(
            active,
            lax.dynamic_update_slice_in_dim(blank, values.astype(jnp.float32), offset, 2),
            0.0,
        )

    contrib = jnp.stack(
        [
            placed(field[:, :, 0, :], row_pos * row_len, col_pos == 0),
            placed(field[:, :, -1, :], row_pos * row_len, col_pos == py_count - 1),
            placed(field[:, :, :, 0], col_pos * col_len, row_pos == 0),
            placed(field[:, :, :, -1], col_pos * col_len, row_pos == px_count - 1),
        ],
        axis=2,
    )
    return lax.psum(contrib.astype(jnp.bfloat16), ("px", "py"))


def pad_field(field, edge_table, corner_table):
    col_len = field.shape[2]
    row_len = field.shape[3]
    row_pos = lax.axis_index("px")
    col_pos = lax.axis_index("py")
    px_count = lax.axis_size("px")
    py_count = lax.axis_size("py")
    padded = with_halo(field, (("px", 3), ("py", 2)), 1)
    lines = face_lines_of(field, row_pos, col_pos, px_count, py_count)
    strips = edge_strips(lines, edge_table, corner_table)
    top_row = lax.dynamic_slice_in_dim(strips[0], row_pos * row_len, row_len + 2, 2)
    bottom_row = lax.dynamic_slice_in_dim(strips[1], row_pos * row_len, row_len + 2, 2)
    left_col = lax.dynamic_slice_in_dim(strips[2], col_pos * col_len, col_len + 2, 2)
    right_col = lax.dynamic_slice_in_dim(strips[3], col_pos * col_len, col_len + 2, 2)
    padded = padded.at[:, :, 0, :].set(jnp.where(col_pos == 0, top_row, padded[:, :, 0, :]))
    padded = padded.at[:, :, -1, :].set(
        jnp.where(col_pos == py_count - 1, bottom_row, padded[:, :, -1, :])
    )
    padded = padded.at[:, :, :, 0].set(jnp.where(row_pos == 0, left_col, padded[:, :, :, 0]))
    padded = padded.at[:, :, :, -1].set(
        jnp.where(row_pos == px_count - 1, right_col, padded[:, :, :, -1])
    )
    return padded


def forward_taps(padded, taps, out_cols, out_rows):
    summed = None
    for tap_row in range(3):
        for tap_col in range(3):
            window = padded[:, :, tap_row : tap_row + out_cols, tap_col : tap_col + out_rows]
            term_val = jnp.einsum(
                "oc,cfab->ofab", taps[tap_row, tap_col], window, preferred_element_type=jnp.float32
            )
            summed = term_val if summed is None else summed + term_val
    return summed


def backward_taps(padded, taps, out_cols, out_rows):
    summed = None
    for tap_row in range(3):
        for tap_col in range(3):
            window = padded[
                :, :, 2 - tap_row : 2 - tap_row + out_cols, 2 - tap_col : 2 - tap_col + out_rows
            ]
            term_val = jnp.einsum(
                "oc,ofab->cfab", taps[tap_row, tap_col], window, preferred_element_type=jnp.float32
            )
            summed = term_val if summed is None else summed + term_val
    return summed


def gate_outputs(preact, cotangent):
    sigmoid_val = jax.nn.sigmoid(preact)
    activation = (preact * sigmoid_val).astype(jnp.bfloat16)
    gated = (
        cotangent.astype(jnp.float32) * sigmoid_val * (1.0 + preact * (1.0 - sigmoid_val))
    ).astype(jnp.bfloat16)
    return (activation, gated)


def local(features, cotangent, weight, edge_table, corner_table):
    chan_block = features.shape[0]
    face_count = features.shape[1]
    tile_len = features.shape[4]
    row_len = RB
    col_len = tile_len // row_len
    features = features.reshape(chan_block, face_count, col_len, row_len)
    cotangent = cotangent.reshape(chan_block, face_count, col_len, row_len)
    ch_pos = lax.axis_index("ch")
    feat_pad = pad_field(features, edge_table, corner_table)
    own_taps = lax.dynamic_slice_in_dim(weight, ch_pos * chan_block, chan_block, 2)
    piece_taps = own_taps
    preact = forward_taps(
        lax.all_gather(feat_pad, "ch", axis=0, tiled=True), piece_taps, col_len, row_len
    )
    activation, gated = gate_outputs(preact, cotangent)
    grad_pad = pad_field(gated, edge_table, corner_table)
    input_taps = lax.dynamic_slice_in_dim(weight, ch_pos * chan_block, chan_block, 3)
    piece_taps = input_taps
    input_grad = backward_taps(
        lax.all_gather(grad_pad, "ch", axis=0, tiled=True), piece_taps, col_len, row_len
    ).astype(jnp.bfloat16)
    out_shape = (chan_block, face_count, 1, 1, tile_len)
    return (activation.reshape(out_shape), input_grad.reshape(out_shape))


def solution(mesh):
    return jax.shard_map(
        local,
        mesh=mesh,
        in_specs=(P("ch", None, "py", "px", None), P("ch", None, "py", "px", None), P(), P(), P()),
        out_specs=(P("ch", None, "py", "px", None), P("ch", None, "py", "px", None)),
        check_vma=False,
    )
```

profile of v0, /device:TPU:1, one launch (start us, length us, event | category | flops | bytes accessed | tf_op | source)
XLA Modules:
  0.0 1055.0 jit_solution(10775510683861696942)
XLA Ops:
  11.2 3.0 copy.696
  16.1 2.7 select_n.196
  18.7 2.7 select_n.200
  23.1 2.6 copy.698
  27.0 7.6 collective-permute-start
  43.8 4.4 collective-permute-start.2
  48.2 2.1 collective-permute-start.3
  50.4 3.1 collective-permute-done.3
  55.8 258.2 %all-reduce.3.cloned.1.call-done = bf16[16,12,4,128]{1,0,3,2:T(8,128)(2,1)} async-done(((bf16[16,12,4,128]{1,0,3,2:T(8,128)(2,1)}), bf16[16,12,4,128]{1,0,3,2:T(8,128)(2,1)}) %all-reduce.3.cloned.1.call-update) | async-done | bytes 196624 | tf_op jit(solution)/shard_map/psum | solution.py:75
  314.0 3.0 copy.702
  325.0 3.8 scatter.30
  332.9 18.3 %scatter.31 = bf16[16,12,18,34]{3,0,2,1:T(8,128)(2,1)S(1)} dynamic-update-slice(bf16[16,12,18,34]{3,0,2,1:T(8,128)(2,1)S(1)} %scatter.30, bf16[16,12,18,1]{3,0,2,1:T(8,128)(2,1)S(1)} %copy.707, s32[]{:T(128)} %constant.235.clone.1, s32[]{:T(128)} %constant.235.clone.1, s32[]{:T(128)} %constant.235.clone.1, s32[]{:T(128)} %constant.249.clone.1) | dynamic-update-slice | bytes 13828 | tf_op jit(solution)/shard_map/scatter | solution.py:97
  354.0 156.7 %all-gather.3.cloned.1.call-done = bf16[128,12,18,34]{3,0,2,1:T(8,128)(2,1)} async-done(((bf16[16,12,18,34]{3,0,2,1:T(8,128)(2,1)}), bf16[128,12,18,34]{3,0,2,1:T(8,128)(2,1)}) %all-gather.3.cloned.1.call-update) | async-done | bytes 1880080 | tf_op jit(solution)/shard_map/all_gather | solution.py:151
  510.7 4.7 fusion.20
  524.6 2.0 fusion.18
  526.6 2.6 fusion.37
  531.6 2.3 copy.725
  536.3 2.1 collective-permute-start.4
  541.0 1.9 select_n.220
  543.0 1.9 select_n.223
  545.6 2.6 copy.727
  551.0 4.7 collective-permute-start.6
  555.7 2.1 collective-permute-start.7
  557.9 3.2 collective-permute-done.7
  561.9 269.6 %all-reduce.5.cloned.1.call-done = bf16[16,12,4,128]{1,0,3,2:T(8,128)(2,1)} async-done(((bf16[16,12,4,128]{1,0,3,2:T(8,128)(2,1)}), bf16[16,12,4,128]{1,0,3,2:T(8,128)(2,1)}) %all-reduce.5.cloned.1.call-update) | async-done | bytes 196624 | tf_op jit(solution)/shard_map/psum | solution.py:75
  831.5 3.0 copy.731
  843.2 3.8 scatter.36
  850.3 18.6 %scatter.39 = bf16[16,12,18,34]{3,0,2,1:T(8,128)(2,1)S(1)} dynamic-update-slice(bf16[16,12,18,34]{3,0,2,1:T(8,128)(2,1)S(1)} %scatter.36, bf16[16,12,18,1]{3,0,2,1:T(8,128)(2,1)S(1)} %copy.735, s32[]{:T(128)} %constant.235.clone.1, s32[]{:T(128)} %constant.235.clone.1, s32[]{:T(128)} %constant.235.clone.1, s32[]{:T(128)} %constant.249.clone.1) | dynamic-update-slice | bytes 13828 | tf_op jit(solution)/shard_map/scatter | solution.py:97
  871.6 156.8 %all-gather.5.cloned.1.call-done = bf16[128,12,18,34]{3,0,2,1:T(8,128)(2,1)} async-done(((bf16[16,12,18,34]{3,0,2,1:T(8,128)(2,1)}), bf16[128,12,18,34]{3,0,2,1:T(8,128)(2,1)}) %all-gather.5.cloned.1.call-update) | async-done | bytes 1880080 | tf_op jit(solution)/shard_map/all_gather | solution.py:158
  1028.4 4.8 fusion.2
  1034.3 1.9 fusion.10
  1044.1 2.3 add_convert_fusion
  (201 shorter events, 80.5 us)
Async XLA Ops:
  7.2 503.5 %copy-start = (bf16[3,3,128,128]{3,2,1,0:T(8,128)(2,1)S(1)}, bf16[3,3,128,128]{3,2,1,0:T(8,128)(2,1)}, u32[]{:S(2)}) copy-start(bf16[3,3,128,128]{3,2,1,0:T(8,128)(2,1)} %param.27) | copy-start | bytes 884740
  7.2 306.9 %all-reduce.3.cloned.1.call-start = ((), (), s32[]{:S(2)}) async-start(), calls=%async_computation | async-start | bytes 4194304 | tf_op jit(solution)/shard_map/psum | solution.py:75
  25.7 11.4 %copy-start.17 = (s32[12,4,3]{0,1,2:T(4,128)S(1)}, s32[12,4,3]{0,1,2:T(4,128)}, u32[]{:S(2)}) copy-start(s32[12,4,3]{0,1,2:T(4,128)} %param.28) | copy-start | bytes 1732
  25.7 12.6 %copy-start.26 = (s32[12,4,2]{0,2,1:T(2,128)S(1)}, s32[12,4,2]{0,2,1:T(2,128)}, u32[]{:S(2)}) copy-start(s32[12,4,2]{0,2,1:T(2,128)} %param.29) | copy-start | bytes 1156
  25.7 485.0 %all-gather.3.cloned.1.call-start = ((), (), s32[]{:S(2)}) async-start(), calls=%async_computation.1 | async-start | bytes 7962624 | tf_op jit(solution)/shard_map/all_gather | solution.py:151
  27.0 12.9 %collective-permute-start = (bf16[16,12,16,1]{2,0,3,1:T(8,128)(2,1)S(1)}, bf16[16,12,16,1]{2,0,3,1:T(8,128)(2,1)S(1)}, u32[]{:S(2)}, u32[]{:S(2)}) collective-permute-start(bf16[16,12,16,1]{2,0,3,1:T(8,128)(2,1)S(1)} %copy.684), channel_id=1, source_target_pairs={{0,64},{64,128},{128,192},{1,65},{65,129},{129,193},{2,66},{66,130... | collective-permute-start | bytes 18440 | tf_op jit(solution)/shard_map/ppermute | solution.py:16
  35.8 5.6 collective-permute-start.1
  43.8 6.7 collective-permute-start.2
  48.2 5.4 collective-permute-start.3
  55.8 262.1 %copy-start.15 = (pred[12]{0:T(512)(128)(4,1)S(1)}, pred[12]{0:T(512)(128)(4,1)}, u32[]{:S(2)}) copy-start(pred[12]{0:T(512)(128)(4,1)} %get-tuple-element.166) | copy-start | bytes 40
  55.8 263.0 %copy-start.13 = (pred[12]{0:T(512)(128)(4,1)S(1)}, pred[12]{0:T(512)(128)(4,1)}, u32[]{:S(2)}) copy-start(pred[12]{0:T(512)(128)(4,1)} %get-tuple-element.164) | copy-start | bytes 40
  317.1 4.6 copy-start.20
  317.1 4.7 copy-start.11
  317.1 4.9 copy-start.22
  319.9 3.6 copy-start.24
  352.2 479.3 %all-reduce.5.cloned.1.call-start = ((), (), s32[]{:S(2)}) async-start(), calls=%async_computation.2 | async-start | bytes 4194304 | tf_op jit(solution)/shard_map/psum | solution.py:75
  510.7 4.8 copy-start.2
  535.1 9.8 copy-start.7
  535.1 10.2 copy-start.6
  536.3 12.0 %collective-permute-start.4 = (bf16[16,12,16,1]{2,0,3,1:T(8,128)(2,1)S(1)}, bf16[16,12,16,1]{2,0,3,1:T(8,128)(2,1)S(1)}, u32[]{:S(2)}, u32[]{:S(2)}) collective-permute-start(bf16[16,12,16,1]{2,0,3,1:T(8,128)(2,1)S(1)} %copy.720), channel_id=1, source_target_pairs={{0,64},{64,128},{128,192},{1,65},{65,129},{129,193},{2,66},{66,130... | collective-permute-start | bytes 18440 | tf_op jit(solution)/shard_map/ppermute | solution.py:16
  539.7 9.9 collective-permute-start.5
  548.3 480.1 %all-gather.5.cloned.1.call-start = ((), (), s32[]{:S(2)}) async-start(), calls=%async_computation.3 | async-start | bytes 7962624 | tf_op jit(solution)/shard_map/all_gather | solution.py:158
  551.0 6.8 collective-permute-start.6
  555.7 5.4 collective-permute-start.7
  561.9 275.6 %copy-start.16 = (pred[12]{0:T(512)(128)(4,1)S(1)}, pred[12]{0:T(512)(128)(4,1)}, u32[]{:S(2)}) copy-start(pred[12]{0:T(512)(128)(4,1)} %get-tuple-element.166) | copy-start | bytes 40
  561.9 275.8 %copy-start.25 = (pred[12]{0:T(512)(128)(4,1)S(1)}, pred[12]{0:T(512)(128)(4,1)}, u32[]{:S(2)}) copy-start(pred[12]{0:T(512)(128)(4,1)} %get-tuple-element.162) | copy-start | bytes 40
  561.9 275.9 %copy-start.14 = (pred[12]{0:T(512)(128)(4,1)S(1)}, pred[12]{0:T(512)(128)(4,1)}, u32[]{:S(2)}) copy-start(pred[12]{0:T(512)(128)(4,1)} %get-tuple-element.164) | copy-start | bytes 40
  561.9 276.1 %copy-start.23 = (pred[12]{0:T(512)(128)(4,1)S(1)}, pred[12]{0:T(512)(128)(4,1)}, u32[]{:S(2)}) copy-start(pred[12]{0:T(512)(128)(4,1)} %get-tuple-element.161) | copy-start | bytes 40
  834.5 5.5 copy-start.21
  834.5 5.6 copy-start.9
  849.0 20.9 %copy-start.5 = (bf16[16,12,16,32]{3,0,2,1:T(8,128)(2,1)S(1)}, bf16[16,12,16,32]{3,0,2,1:T(8,128)(2,1)}, u32[]{:S(2)}) copy-start(bf16[16,12,16,32]{3,0,2,1:T(8,128)(2,1)} %get-tuple-element.139) | copy-start | bytes 589828
  1028.4 4.8 copy-start.1
  (7 other events, 13.3 us)
Sparse Core Ops, SparseCore 0:
  25.8 288.1 all-reduce.2
  352.3 158.3 all-gather.2
  548.4 283.0 all-reduce.4
  870.0 158.3 all-gather.4
where the time goes:
time: 1060 us
  waiting for transfers between devices  848 us (80%)
  local copies, waits for them, and re-layouts  117 us (11%)
  matrix products  36.3 us (3%)
  starting transfers between devices  26.2 us (2%)
  between operations  15.3 us (1%)
  other arithmetic  12.9 us (1%)
    psum x2, waiting for transfers between devices, face_lines_of(): return lax.psum(contrib.astype(jnp.bfloat16), ('px', 'py'))  528 us
    all_gather x1, waiting for transfers between devices, local(): lax.all_gather(grad_pad, 'ch', axis=0, tiled=True)  157 us
    all_gather x1, waiting for transfers between devices, local(): lax.all_gather(feat_pad, 'ch', axis=0, tiled=True)  157 us
    scatter x2, local copies, waits for them, and re-layouts, pad_field(): padded.at[:, :, :, -1]  36.9 us
  transfers between devices with their start and end apart: 12, of which 6 were waited for; matrix products, arithmetic and copies ran while one was open for 2% of the time, Pallas kernels for 0%

commit v1 on v0

v1 whole, which is shorter than its diff:
```python
import functools

import jax
import jax.numpy as jnp
from jax import lax
from jax.experimental import pallas as pl
from jax.experimental.pallas import tpu as pltpu
from jax.sharding import PartitionSpec as P

MESH = pl.DeviceIdType.MESH
F32 = jnp.float32
BF16 = jnp.bfloat16
FACES, CB, RA, RB, TILE = 12, 16, 16, 32, 512
N_PX, N_PY, N_X, N_Z = 4, 8, 4, 2
SIDE = 128
RING = 128
WIDE = TILE + RING

TOP, BOTTOM, LEFT, RIGHT = 0, 34, 68, 84
HALO = (
    (0, 1, 1, 0),
    (0, -1, 0, 1),
    (1, 0, 2, 2),
    (-1, 0, 2, 3),
    (1, 1, 1, 4),
    (-1, 1, 1, 5),
    (1, -1, 0, 6),
    (-1, -1, 0, 7),
)


def iota(shape, dim):
    return lax.broadcasted_iota(jnp.int32, shape, dim)


def ones_where(mask):
    return jnp.where(mask, 1.0, 0.0).astype(BF16)


def dot(a, b):
    return jnp.dot(a, b, preferred_element_type=F32)


def fill_selectors(sbd, sring, sline, scol, sconv):
    p, n = iota((TILE, 128), 0), iota((TILE, 128), 1)
    i = n % 32
    for kind in range(3):
        if kind == 0:
            src = i
        elif kind == 1:
            src = (RA - 1) * RB + i
        else:
            src = jnp.where(i < 16, RB * i, RB * (i - 16) + RB - 1)
        hit = p == src
        for k in range(4):
            sbd[k, :, 128 * kind : 128 * kind + 128] = ones_where(hit & (n // 32 == k))
    row, m = iota((128, 128), 0), iota((128, 128), 1)
    k, i = row // 32, row % 32
    aims = (
        TOP + 1 + i,
        BOTTOM + 1 + i,
        jnp.where(i >= 16, LEFT + i - 16, -1),
        jnp.where(i < 16, RIGHT + i, -1),
        jnp.where(i == 31, TOP, -1),
        jnp.where(i == 0, TOP + 33, -1),
        jnp.where(i == 31, BOTTOM, -1),
        jnp.where(i == 0, BOTTOM + 33, -1),
    )
    for slot, aim in enumerate(aims):
        for face in range(4):
            sring[128 * slot : 128 * slot + 128, 128 * face : 128 * face + 128] = ones_where(
                (k == face) & (m == aim)
            )
    for face in range(4):
        for q in range(N_PX):
            sline[128 * q : 128 * q + 128, 128 * face : 128 * face + 128] = ones_where(
                (k == face) & (m == 32 * q + i)
            )
        for q in range(N_PY):
            for far in range(2):
                part = (i >= 16) if far else (i < 16)
                scol[far, 128 * q : 128 * q + 128, 128 * face : 128 * face + 128] = ones_where(
                    (k == face) & part & (m == 16 * q + i - 16 * far)
                )
    lane, p = iota((128, TILE), 0), iota((128, TILE), 1)
    for tap in range(9):
        pa, pb = p // RB + tap // 3, p % RB + tap % 3
        cell = jnp.where(
            pa == 0,
            TOP + pb,
            jnp.where(
                pa == RA + 1,
                BOTTOM + pb,
                jnp.where(pb == 0, LEFT + pa - 1, jnp.where(pb == RB + 1, RIGHT + pa - 1, -1)),
            ),
        )
        sconv[128 * tap : 128 * tap + 128, :] = ones_where(lane == cell)


def kernel(
    edge_ref,
    corner_ref,
    feat_ref,
    cot_ref,
    w_ref,
    act_ref,
    grad_ref,
    held,
    bd,
    hal,
    lin,
    full,
    ring,
    pre,
    ringy,
    gated,
    wst,
    sbd,
    sring,
    sline,
    scol,
    sconv,
    ag_send,
    ag_recv,
    halo_send,
    halo_recv,
    line_send,
    line_recv,
):
    px, py, ch = lax.axis_index("px"), lax.axis_index("py"), lax.axis_index("ch")
    z, x = ch // N_X, ch % N_X
    up_x = z * N_X + (x + 1) % N_X
    down_x = z * N_X + (x + N_X - 1) % N_X
    far = (1 - z) * N_X + x
    far_up = (1 - z) * N_X + (x + 1) % N_X
    far_down = (1 - z) * N_X + (x + N_X - 1) % N_X

    def on_border(qx, qy):
        return (qx == 0) | (qx == N_PX - 1) | (qy == 0) | (qy == N_PY - 1)

    border = on_border(px, py)
    sides = (py == 0, py == N_PY - 1, px == 0, px == N_PX - 1)

    barrier = pltpu.get_barrier_semaphore()

    def greet(t, carry):
        tx, ty = t // N_PY, t % N_PY

        @pl.when((tx != px) | (ty != py))
        def _():
            pl.semaphore_signal(barrier, inc=1, device_id={"px": tx, "py": ty}, device_id_type=MESH)

        return carry

    lax.fori_loop(0, N_PX * N_PY, greet, 0)
    for peer in (far, up_x, down_x):
        pl.semaphore_signal(barrier, inc=1, device_id={"ch": peer}, device_id_type=MESH)

    fill_selectors(sbd, sring, sline, scol, sconv)
    pick = ones_where(iota((CB, 128), 1) == CB * ch + iota((CB, 128), 0))
    for tap in range(9):
        wst[0, CB * tap : CB * tap + CB, :] = w_ref[tap, pl.ds(pl.multiple_of(CB * ch, CB), CB), :]
        wst[1, CB * tap : CB * tap + CB, :] = lax.dot_general(
            pick, w_ref[8 - tap], (((1,), (1,)), ((), ())), preferred_element_type=F32
        ).astype(BF16)
    for s in range(2):
        for dx, dy, kind, slot in HALO:
            sx, sy = px - dx, py - dy

            @pl.when((sx < 0) | (sx >= N_PX) | (sy < 0) | (sy >= N_PY))
            def _():
                hal[s, slot] = jnp.zeros((3 * CB, 128), BF16)

    pl.semaphore_wait(barrier, N_PX * N_PY - 1 + 3)

    def rows(c):
        return pl.ds(pl.multiple_of(CB * c, CB), CB)

    def ag_copy(s, kind, index):
        block, target, faces = (
            (ch, far, (0, 12)),
            (ch, up_x, (0, 12)),
            (ch, down_x, (0, 12)),
            (far, up_x, (0, 12)),
            (far, down_x, (0, 12)),
            (down_x, up_x, (0, 6)),
            (up_x, down_x, (6, 12)),
            (far_down, up_x, (0, 6)),
            (far_up, down_x, (6, 12)),
        )[index]
        lanes = pl.ds(0, TILE) if kind == 0 else pl.ds(TILE, RING)
        ref = held.at[s, pl.ds(faces[0], faces[1] - faces[0]), rows(block), lanes]
        return pltpu.make_async_remote_copy(
            src_ref=ref,
            dst_ref=ref,
            send_sem=ag_send.at[s, kind, index],
            recv_sem=ag_recv.at[s, kind, index],
            device_id={"ch": target},
            device_id_type=MESH,
        )

    def halo_copy(s, n):
        dx, dy, kind, slot = HALO[n]
        return pltpu.make_async_remote_copy(
            src_ref=bd.at[s, kind],
            dst_ref=hal.at[s, slot],
            send_sem=halo_send.at[s, slot],
            recv_sem=halo_recv.at[s, slot],
            device_id={"px": px + dx, "py": py + dy},
            device_id_type=MESH,
        )

    def inside(qx, qy):
        return (qx >= 0) & (qx < N_PX) & (qy >= 0) & (qy < N_PY)

    my_slots = (px, N_PX + px, 2 * N_PX + py, 2 * N_PX + N_PY + py)

    def line_copy(s, side, t):
        return pltpu.make_async_remote_copy(
            src_ref=bd.at[s, min(side, 2)],
            dst_ref=lin.at[s, my_slots[side]],
            send_sem=line_send.at[s, side, t],
            recv_sem=line_recv.at[s, my_slots[side]],
            device_id={"px": t // N_PY, "py": t % N_PY},
            device_id_type=MESH,
        )

    def each_line_copy(s, act):
        for side in range(4):

            @pl.when(sides[side])
            def _():
                def one(t, carry):
                    tx, ty = t // N_PY, t % N_PY

                    @pl.when(on_border(tx, ty) & ((tx != px) | (ty != py)))
                    def _():
                        act(line_copy(s, side, t))

                    return carry

                lax.fori_loop(0, N_PX * N_PY, one, 0)

    def make_ring(s):
        cells = jnp.concatenate([hal[s, slot] for slot in range(8)], axis=1)
        inner = dot(cells, sring[...])
        for q in range(3):
            for k in range(4):
                ring[4 * q + k] = inner[CB * q : CB * q + CB, 128 * k : 128 * k + 128]

        @pl.when(border)
        def _():
            for side in range(4):
                first, count = ((0, 4), (4, 4), (8, 8), (16, 8))[side]
                parts = jnp.concatenate([lin[s, first + q] for q in range(count)], axis=1)
                table = sline[...] if side < 2 else scol[side - 2]
                lines = dot(parts, table).astype(BF16)
                for q in range(3):
                    for k in range(4):
                        full[12 * side + 4 * q + k] = lines[
                            CB * q : CB * q + CB, 128 * k : 128 * k + 128
                        ]
            t, n = iota((128, 128), 0), iota((128, 128), 1)
            for edge in range(4):

                @pl.when(sides[edge])
                def _():
                    none = jnp.full((128, 128), -1000, jnp.int32)
                    if edge < 2:
                        base = (TOP, BOTTOM)[edge]
                        at = jnp.where(
                            (n >= base) & (n < base + 34), RB * px - 1 + n - base, none
                        )
                    else:
                        base = (LEFT, RIGHT)[edge - 2]
                        shift = 33 * (edge - 2)
                        at = jnp.where((n >= base) & (n < base + 16), RA * py + n - base, none)
                        at = jnp.where(n == TOP + shift, RA * py - 1, at)
                        at = jnp.where(n == BOTTOM + shift, RA * py + RA, at)

                    def face_edge(f, carry):
                        e = 12 * f + 3 * edge
                        line = full[12 * edge_ref[e + 1] + edge_ref[e]]
                        src = jnp.where(edge_ref[e + 2] == 1, SIDE - 1 - at, at)
                        ring[f] += dot(line, ones_where(t == src))
                        return carry

                    lax.fori_loop(0, FACES, face_edge, 0)

            for corner in range(4):
                lane = (TOP, TOP + 33, BOTTOM, BOTTOM + 33)[corner]

                @pl.when(sides[corner // 2] & sides[2 + corner % 2])
                def _():
                    def face_corner(f, carry):
                        c = 8 * f + 2 * corner
                        q = corner_ref[c + 1]
                        line = full[12 * (q // 2) + corner_ref[c]]
                        hit = (t == (SIDE - 1) * (q % 2)) & (n == lane)
                        ring[f] += dot(line, ones_where(hit))
                        return carry

                    lax.fori_loop(0, FACES, face_corner, 0)

        held[s, :, rows(ch), TILE:WIDE] = ring[...].astype(BF16)

    def gather(s, v_ref):
        held[s, :, rows(ch), 0:TILE] = v_ref[...]
        for index in range(3):
            ag_copy(s, 0, index).start()
        packed = None
        for k in range(4):
            part = jnp.concatenate([v_ref[4 * q + k] for q in range(3)], axis=0)
            term = dot(part, sbd[k])
            packed = term if packed is None else packed + term
        packed = packed.astype(BF16)
        for kind in range(3):
            bd[s, kind] = packed[:, 128 * kind : 128 * kind + 128]
        for n, (dx, dy, kind, slot) in enumerate(HALO):

            @pl.when(inside(px + dx, py + dy))
            def _():
                halo_copy(s, n).start()

        for side in range(4):

            @pl.when(sides[side])
            def _():
                lin[s, my_slots[side]] = bd[s, min(side, 2)]

        each_line_copy(s, lambda copy: copy.start())

        for n, (dx, dy, kind, slot) in enumerate(HALO):

            @pl.when(inside(px - dx, py - dy))
            def _():
                halo_copy(s, n).wait_recv()

        @pl.when(border)
        def _():
            def arrived(j, first, qx, qy):
                @pl.when((qx != px) | (qy != py))
                def _():
                    pltpu.make_async_remote_copy(
                        src_ref=bd.at[s, 0],
                        dst_ref=lin.at[s, j],
                        send_sem=line_send.at[s, 0, 0],
                        recv_sem=line_recv.at[s, j],
                        device_id={"px": px, "py": py},
                        device_id_type=MESH,
                    ).wait_recv()

            for q in range(N_PX):
                arrived(q, 0, q, 0)
                arrived(N_PX + q, 0, q, N_PY - 1)
            for q in range(N_PY):
                arrived(2 * N_PX + q, 0, 0, q)
                arrived(2 * N_PX + N_PY + q, 0, N_PX - 1, q)

        make_ring(s)
        for index in range(3):
            ag_copy(s, 1, index).start()
        for kind in range(2):
            for index in (1, 2):
                ag_copy(s, kind, index).wait_recv()
            for index in (5, 6):
                ag_copy(s, kind, index).start()
        for kind in range(2):
            ag_copy(s, kind, 0).wait_recv()
            for index in (3, 4):
                ag_copy(s, kind, index).start()
        for kind in range(2):
            for index in (3, 4):
                ag_copy(s, kind, index).wait_recv()
            for index in (7, 8):
                ag_copy(s, kind, index).start()
        for kind in range(2):
            for index in (5, 6, 7, 8):
                ag_copy(s, kind, index).wait_recv()

    def convolve(s):
        p = iota((CB, TILE), 1)
        a, b = p // RB, p % RB
        keep_a = (a >= 1, None, a < RA - 1)
        keep_b = (b >= 1, None, b < RB - 1)

        def face_conv(f, carry):
            y = dot(wst[s], held[s, f])
            total = None
            for dj in range(3):
                column = None
                for di in range(3):
                    tap = 3 * di + dj
                    term = y[CB * tap : CB * tap + CB, 0:TILE]
                    if di != 1:
                        term = pltpu.roll(term, (-(di - 1) * RB) % TILE, 1)
                        term = jnp.where(keep_a[di], term, 0.0)
                    column = term if column is None else column + term
                if dj != 1:
                    column = pltpu.roll(column, (-(dj - 1)) % TILE, 1)
                    column = jnp.where(keep_b[dj], column, 0.0)
                total = column if total is None else total + column
            pre[f] = total
            edge = jnp.concatenate(
                [y[CB * tap : CB * tap + CB, TILE:WIDE] for tap in range(9)], axis=1
            )
            high = edge.astype(BF16)
            ringy[f, 0:CB, :] = high
            ringy[f, CB : 2 * CB, :] = (edge - high.astype(F32)).astype(BF16)
            return carry

        lax.fori_loop(0, FACES, face_conv, 0)

        def add_ring(g, carry):
            first = pl.multiple_of(4 * g, 4)
            cells = ringy[pl.ds(first, 4)].reshape(8 * CB, 9 * RING)
            extra = dot(cells, sconv[...]).reshape(4, 2, CB, TILE)
            pre[pl.ds(first, 4)] += extra[:, 0] + extra[:, 1]
            return carry

        lax.fori_loop(0, FACES // 4, add_ring, 0)

    gather(0, feat_ref)
    convolve(0)

    def gate(f, carry):
        v = pre[f]
        sig = 1.0 / (1.0 + jnp.exp(-v))
        act_ref[f] = (v * sig).astype(BF16)
        gated[f] = (cot_ref[f].astype(F32) * sig * (1.0 + v * (1.0 - sig))).astype(BF16)
        return carry

    lax.fori_loop(0, FACES, gate, 0)
    gather(1, gated)
    convolve(1)

    def finish(f, carry):
        grad_ref[f] = pre[f].astype(BF16)
        return carry

    lax.fori_loop(0, FACES, finish, 0)

    for s in range(2):
        for kind in range(2):
            for index in range(9):
                ag_copy(s, kind, index).wait_send()
        for n, (dx, dy, kind, slot) in enumerate(HALO):

            @pl.when(inside(px + dx, py + dy))
            def _():
                halo_copy(s, n).wait_send()

        each_line_copy(s, lambda copy: copy.wait_send())


def local(features, cotangent, weight, edge_table, corner_table):
    def by_face(v):
        return jnp.transpose(v.reshape(CB, FACES, TILE), (1, 0, 2))

    vmem = pl.BlockSpec(memory_space=pltpu.VMEM)
    smem = pl.BlockSpec(memory_space=pltpu.SMEM)
    field = jax.ShapeDtypeStruct((FACES, CB, TILE), BF16)
    act, grad = pl.pallas_call(
        kernel,
        out_shape=(field, field),
        in_specs=[smem, smem, vmem, vmem, vmem],
        out_specs=(vmem, vmem),
        scratch_shapes=[
            pltpu.VMEM((2, FACES, 8 * CB, WIDE), BF16),
            pltpu.VMEM((2, 3, 3 * CB, 128), BF16),
            pltpu.VMEM((2, 8, 3 * CB, 128), BF16),
            pltpu.VMEM((2, 24, 3 * CB, 128), BF16),
            pltpu.VMEM((48, CB, 128), BF16),
            pltpu.VMEM((FACES, CB, RING), F32),
            pltpu.VMEM((FACES, CB, TILE), F32),
            pltpu.VMEM((FACES, 2 * CB, 9 * RING), BF16),
            pltpu.VMEM((FACES, CB, TILE), BF16),
            pltpu.VMEM((2, 9 * CB, 128), BF16),
            pltpu.VMEM((4, TILE, 384), BF16),
            pltpu.VMEM((1024, 512), BF16),
            pltpu.VMEM((512, 512), BF16),
            pltpu.VMEM((2, 1024, 512), BF16),
            pltpu.VMEM((9 * RING, TILE), BF16),
            pltpu.SemaphoreType.DMA((2, 2, 9)),
            pltpu.SemaphoreType.DMA((2, 2, 9)),
            pltpu.SemaphoreType.DMA((2, 8)),
            pltpu.SemaphoreType.DMA((2, 8)),
            pltpu.SemaphoreType.DMA((2, 4, N_PX * N_PY)),
            pltpu.SemaphoreType.DMA((2, 24)),
        ],
        compiler_params=pltpu.CompilerParams(
            collective_id=0, has_side_effects=True, vmem_limit_bytes=48 * 1024 * 1024
        ),
        name="conv_pair",
    )(
        edge_table.reshape(-1),
        corner_table.reshape(-1),
        by_face(features),
        by_face(cotangent),
        weight.reshape(9, 8 * CB, 8 * CB),
    )

    def by_channel(v):
        return jnp.transpose(v, (1, 0, 2)).reshape(CB, FACES, 1, 1, TILE)

    return by_channel(act), by_channel(grad)


def solution(mesh):
    field = P("ch", None, "py", "px", None)
    return jax.shard_map(
        local,
        mesh=mesh,
        in_specs=(field, field, P(), P(), P()),
        out_specs=(field, field),
        check_vma=False,
    )
```

time: 1060 us -> 103 us (0.10)
  the two profiles are of different devices: /device:TPU:1 before, /device:TPU:2 now
where the time goes in v1:
time: 103 us
  Pallas kernels  96.5 us (94%)
  local copies, waits for them, and re-layouts  5.89 us (6%)
    pallas_call x1, Pallas kernels, local(): pl.pallas_call(kernel, out_shape=(field, field), in_specs=[smem, smem, vm...  96.5 us
    unnamed x12, local copies, waits for them, and re-layouts  5.64 us

profile of v1, /device:TPU:2, one launch (start us, length us, event | category | flops | bytes accessed | tf_op | source)
XLA Modules:
  0.0 103.0 jit_solution(7233828442149750947)
XLA Ops:
  0.6 0.8 copy.10
  1.4 0.0 copy-start.3
  1.4 0.1 reshape.25.edge_ref
  1.6 0.6 copy-done.3
  2.1 0.1 copy.11
  2.2 0.1 reshape.26.corner_ref
  2.4 0.0 copy-start
  2.4 1.0 copy-done
  3.3 0.0 copy-start.1
  3.3 0.9 copy-done.1
  4.3 0.0 copy-start.2
  4.3 0.9 copy-done.2
  5.2 96.5 %conv_pair.1 = (bf16[12,16,512]{2,1,0:T(8,128)(2,1)S(1)}, bf16[12,16,512]{2,1,0:T(8,128)(2,1)S(1)}) custom-call(s32[144]{0:T(256)S(1)} %reshape.25.edge_ref, s32[96]{0:T(128)S(1)} %reshape.26.corner_ref, bf16[12,16,512]{2,1,0:T(8,128)(2,1)S(1)} %bitcast.20, bf16[12,16,512]{2,1,0:T(8,128)(2,1)S(1)} %bitcast.21, bf16[9,128,128]{2,1,0:T(8,128)(2,1)S(1)} %bitcast.17), custom_call_target="tpu_custom_call" | custom-call | tf_op jit(solution)/shard_map/conv_pair/pallas_call | solution.py:463
  101.7 0.7 copy.16
  102.4 0.7 copy.17
Async XLA Ops:
  1.4 0.7 copy-start.3
  2.4 1.0 copy-start
  3.3 0.9 copy-start.1
  4.3 0.9 copy-start.2

commit v2 on v1

v2 whole, which is shorter than its diff:
```python
import functools

import jax
import jax.numpy as jnp
from jax import lax
from jax.experimental import pallas as pl
from jax.experimental.pallas import tpu as pltpu
from jax.sharding import PartitionSpec as P

MESH = pl.DeviceIdType.MESH
F32 = jnp.float32
BF16 = jnp.bfloat16
FACES, CB, RA, RB, TILE = 12, 16, 16, 32, 512
N_PX, N_PY, N_X, N_Z = 4, 8, 4, 2
SIDE = 128
RING = 128
WIDE = TILE + RING

TOP, BOTTOM, LEFT, RIGHT = 0, 34, 68, 84
HALO = (
    (0, 1, 1, 0),
    (0, -1, 0, 1),
    (1, 0, 2, 2),
    (-1, 0, 2, 3),
    (1, 1, 1, 4),
    (-1, 1, 1, 5),
    (1, -1, 0, 6),
    (-1, -1, 0, 7),
)
BORDER = tuple(
    (qx, qy)
    for qx in range(N_PX)
    for qy in range(N_PY)
    if qx in (0, N_PX - 1) or qy in (0, N_PY - 1)
)
SLOTS = 2 * N_PX + 2 * N_PY
PART = 3
PARTS = FACES // PART
Z, XU, XD, FU, FD, ZU, ZD, ZF = 0, 4, 5, 6, 7, 8, 12, 16


def iota(shape, dim):
    return lax.broadcasted_iota(jnp.int32, shape, dim)


def ones_where(mask):
    return jnp.where(mask, 1.0, 0.0).astype(BF16)


def dot(a, b):
    return jnp.dot(a, b, preferred_element_type=F32)


def fill_packers(px, py, sbd):
    p, n = iota((TILE, 128), 0), iota((TILE, 128), 1)
    i, j = n % 32, (n // 32 - px) & 3
    for kind in range(2):
        hit = p == (RA - 1) * RB * kind + i
        for k in range(4):
            sbd[k, :, 128 * kind : 128 * kind + 128] = ones_where(hit & (j == k))
    i, m = n % 16, (n // 16 - py) & 7
    hit = p == RB * i + jnp.where(m >= 4, RB - 1, 0)
    for k in range(4):
        sbd[k, :, 256:384] = ones_where(hit & ((m & 3) == k))


def fill_selectors(px, py, sring, sedge, scorner, sconv):
    row, m = iota((128, 128), 0), iota((128, 128), 1)
    i, j = row % 32, row // 32
    i16, item = row % 16, (row // 16 - py) & 7
    here, left, right = (j - px) & 3, (j - px + 1) & 3, (j - px - 1) & 3
    aims = (
        (here, TOP + 1 + i),
        (here, BOTTOM + 1 + i),
        (item & 3, jnp.where(item >= 4, LEFT + i16, -1)),
        (item & 3, jnp.where(item < 4, RIGHT + i16, -1)),
        (left, jnp.where(i == 31, TOP, -1)),
        (right, jnp.where(i == 0, TOP + 33, -1)),
        (left, jnp.where(i == 31, BOTTOM, -1)),
        (right, jnp.where(i == 0, BOTTOM + 33, -1)),
    )
    for slot, (k, aim) in enumerate(aims):
        for face in range(4):
            sring[128 * slot : 128 * slot + 128, 128 * face : 128 * face + 128] = ones_where(
                (k == face) & (m == aim)
            )
    none = jnp.full((128, 128), -1000, jnp.int32)
    for edge in range(4):
        if edge < 2:
            base = (TOP, BOTTOM)[edge]
            at = jnp.where((m >= base) & (m < base + 34), RB * px - 1 + m - base, none)
        else:
            base, shift = (LEFT, RIGHT)[edge - 2], 33 * (edge - 2)
            at = jnp.where((m >= base) & (m < base + 16), RA * py + m - base, none)
            at = jnp.where(m == TOP + shift, RA * py - 1, at)
            at = jnp.where(m == BOTTOM + shift, RA * py + RA, at)
        sedge[edge, :, 0:128] = ones_where(row == at)
        sedge[edge, :, 128:256] = ones_where(row == SIDE - 1 - at)
        cell = m == (TOP, TOP + 33, BOTTOM, BOTTOM + 33)[edge]
        scorner[edge, :, 0:128] = ones_where(cell & (row == 0))
        scorner[edge, :, 128:256] = ones_where(cell & (row == SIDE - 1))
    lane, p = iota((128, TILE), 0), iota((128, TILE), 1)
    for tap in range(9):
        pa, pb = p // RB + tap // 3, p % RB + tap % 3
        cell = jnp.where(
            pa == 0,
            TOP + pb,
            jnp.where(
                pa == RA + 1,
                BOTTOM + pb,
                jnp.where(pb == 0, LEFT + pa - 1, jnp.where(pb == RB + 1, RIGHT + pa - 1, -1)),
            ),
        )
        sconv[128 * tap : 128 * tap + 128, :] = ones_where(lane == cell)


def kernel(
    edge_ref,
    corner_ref,
    feat_ref,
    cot_hbm,
    w_hbm,
    act_ref,
    grad_ref,
    held,
    cot_ref,
    w_ref,
    bd,
    hal,
    lin,
    full,
    ring,
    pre,
    ringy,
    wst,
    sbd,
    sring,
    sedge,
    scorner,
    sconv,
    load_sem,
    ag_send,
    ag_recv,
    rg_send,
    rg_recv,
    halo_send,
    halo_recv,
    line_send,
    line_recv,
):
    px, py, ch = lax.axis_index("px"), lax.axis_index("py"), lax.axis_index("ch")
    z, x = ch // N_X, ch % N_X
    up_x = z * N_X + (x + 1) % N_X
    down_x = z * N_X + (x + N_X - 1) % N_X
    far = (1 - z) * N_X + x
    far_up = (1 - z) * N_X + (x + 1) % N_X
    far_down = (1 - z) * N_X + (x + N_X - 1) % N_X
    sides = (py == 0, py == N_PY - 1, px == 0, px == N_PX - 1)
    border = sides[0] | sides[1] | sides[2] | sides[3]
    at_corner = (sides[0] | sides[1]) & (sides[2] | sides[3])

    def rows(c):
        return pl.ds(pl.multiple_of(CB * c, CB), CB)

    loads = (
        pltpu.make_async_copy(feat_ref, held.at[0, :, rows(ch), pl.ds(0, TILE)], load_sem.at[0]),
        pltpu.make_async_copy(w_hbm, w_ref, load_sem.at[1]),
        pltpu.make_async_copy(cot_hbm, cot_ref, load_sem.at[2]),
    )
    for load in loads:
        load.start()

    barrier = pltpu.get_barrier_semaphore()

    def greet(t, carry):
        tx, ty = t // N_PY, t % N_PY

        @pl.when((tx != px) | (ty != py))
        def _():
            pl.semaphore_signal(barrier, inc=1, device_id={"px": tx, "py": ty}, device_id_type=MESH)

        return carry

    lax.fori_loop(0, N_PX * N_PY, greet, 0)
    for peer in (far, up_x, down_x):
        pl.semaphore_signal(barrier, inc=1, device_id={"ch": peer}, device_id_type=MESH)

    def pack(s):
        packed = None
        for k in range(4):
            part = jnp.concatenate(
                [held[s, 4 * q + k, rows(ch), 0:TILE] for q in range(3)], axis=0
            )
            term = dot(part, sbd[k])
            packed = term if packed is None else packed + term
        packed = packed.astype(BF16)
        for kind in range(3):
            bd[s, kind] = packed[:, 128 * kind : 128 * kind + 128]

    fill_packers(px, py, sbd)
    loads[0].wait()
    pack(0)
    fill_selectors(px, py, sring, sedge, scorner, sconv)
    loads[1].wait()
    pick_row = ones_where(iota((CB, 128), 1) == CB * ch + iota((CB, 128), 0))
    for tap in range(9):
        wst[0, CB * tap : CB * tap + CB, :] = w_ref[tap, rows(ch), :]
        wst[1, CB * tap : CB * tap + CB, :] = lax.dot_general(
            pick_row, w_ref[8 - tap], (((1,), (1,)), ((), ())), preferred_element_type=F32
        ).astype(BF16)
    for s in range(2):
        for dx, dy, kind, slot in HALO:
            sx, sy = px - dx, py - dy

            @pl.when((sx < 0) | (sx >= N_PX) | (sy < 0) | (sy >= N_PY))
            def _():
                hal[s, slot] = jnp.zeros((3 * CB, 128), BF16)

    loads[2].wait()
    pl.semaphore_wait(barrier, N_PX * N_PY - 1 + 3)

    def remote(ref, send, recv, device, dst=None):
        return pltpu.make_async_remote_copy(
            src_ref=ref,
            dst_ref=ref if dst is None else dst,
            send_sem=send,
            recv_sem=recv,
            device_id=device,
            device_id_type=MESH,
        )

    def ag_copy(s, index):
        if index < XU:
            block, target, first, count = ch, far, PART * index, PART
        elif index < ZU:
            block, target, first, count = (
                (ch, up_x, 0, FACES),
                (ch, down_x, 0, FACES),
                (down_x, up_x, 0, FACES // 2),
                (up_x, down_x, FACES // 2, FACES // 2),
            )[index - XU]
        elif index < ZF:
            part = (index - ZU) % 4
            block, target = far, up_x if index < ZD else down_x
            first, count = PART * part, PART
        else:
            part = index - ZF
            block, target = (far_down, up_x) if part < 2 else (far_up, down_x)
            first, count = PART * part, PART
        ref = held.at[s, pl.ds(first, count), rows(block), pl.ds(0, TILE)]
        return remote(ref, ag_send.at[s, index], ag_recv.at[s, index], {"ch": target})

    def rg_copy(s, index):
        block, target, first, count = (
            (ch, far, 0, 12),
            (ch, up_x, 0, 12),
            (ch, down_x, 0, 12),
            (far, up_x, 0, 12),
            (far, down_x, 0, 12),
            (down_x, up_x, 0, 6),
            (up_x, down_x, 6, 6),
            (far_down, up_x, 0, 6),
            (far_up, down_x, 6, 6),
        )[index]
        ref = held.at[s, pl.ds(first, count), rows(block), pl.ds(TILE, RING)]
        return remote(ref, rg_send.at[s, index], rg_recv.at[s, index], {"ch": target})

    def halo_copy(s, n):
        dx, dy, kind, slot = HALO[n]
        return remote(
            bd.at[s, kind],
            halo_send.at[s, slot],
            halo_recv.at[s, slot],
            {"px": px + dx, "py": py + dy},
            hal.at[s, slot],
        )

    def inside(qx, qy):
        return (qx >= 0) & (qx < N_PX) & (qy >= 0) & (qy < N_PY)

    my_slots = (px, N_PX + px, 2 * N_PX + py, 2 * N_PX + N_PY + py)

    def many_lines(s, count, send, recv):
        ref = lin.at[s, pl.ds(0, count)]
        return remote(ref, send, recv, {"px": px, "py": py})

    def send_lines(s):
        for side in range(4):

            @pl.when(sides[side])
            def _():
                for tx, ty in BORDER:

                    @pl.when((px != tx) | (py != ty))
                    def _():
                        remote(
                            bd.at[s, min(side, 2)],
                            line_send.at[s, side],
                            line_recv.at[s],
                            {"px": tx, "py": ty},
                            lin.at[s, my_slots[side]],
                        ).start()

                lin[s, my_slots[side]] = bd[s, min(side, 2)]

    def take_lines(s):
        @pl.when(at_corner)
        def _():
            many_lines(s, SLOTS - 2, line_send.at[s, 0], line_recv.at[s]).wait_recv()

        @pl.when(border & jnp.logical_not(at_corner))
        def _():
            many_lines(s, SLOTS - 1, line_send.at[s, 0], line_recv.at[s]).wait_recv()

    def make_ring(s):
        cells = jnp.concatenate([hal[s, slot] for slot in range(8)], axis=1)
        inner = dot(cells, sring[...])
        for q in range(3):
            for k in range(4):
                ring[4 * q + k] = inner[CB * q : CB * q + CB, 128 * k : 128 * k + 128]

        @pl.when(border)
        def _():
            lane = iota((3 * CB, 128), 1)
            for side in range(4):
                first, count, width, item = (
                    (0, N_PX, 32, 0),
                    (N_PX, N_PX, 32, 0),
                    (2 * N_PX, N_PY, 16, 0),
                    (2 * N_PX + N_PY, N_PY, 16, 4),
                )[side]
                parts = [lin[s, first + q].astype(F32) for q in range(count)]
                for k in range(4):
                    line = parts[0]
                    for q in range(1, count):
                        line = jnp.where(
                            lane // width == (item + k + q) % count, parts[q], line
                        )
                    turn = (-width * (item + k)) % 128
                    if turn:
                        line = pltpu.roll(line, turn, 1)
                    line = line.astype(BF16)
                    for q in range(3):
                        full[12 * side + 4 * q + k] = line[CB * q : CB * q + CB, :]
            for edge in range(4):

                @pl.when(sides[edge])
                def _():
                    found = jnp.concatenate(
                        [full[12 * edge_ref[1, edge, f] + edge_ref[0, edge, f]] for f in range(FACES)],
                        axis=0,
                    )
                    both = dot(found, sedge[edge])
                    for f in range(FACES):
                        mine = both[CB * f : CB * f + CB]
                        ring[f] += jnp.where(
                            edge_ref[2, edge, f] == 1, mine[:, 128:256], mine[:, 0:128]
                        )

            for corner in range(4):

                @pl.when(sides[corner // 2] & sides[2 + corner % 2])
                def _():
                    found = jnp.concatenate(
                        [
                            full[12 * (corner_ref[corner, 1, f] // 2) + corner_ref[corner, 0, f]]
                            for f in range(FACES)
                        ],
                        axis=0,
                    )
                    both = dot(found, scorner[corner])
                    for f in range(FACES):
                        mine = both[CB * f : CB * f + CB]
                        ring[f] += jnp.where(
                            corner_ref[corner, 1, f] % 2 == 1, mine[:, 128:256], mine[:, 0:128]
                        )

        held[s, :, rows(ch), TILE:WIDE] = ring[...].astype(BF16)

    p = iota((CB, TILE), 1)
    a, b = p // RB, p % RB
    keep_a = (a >= 1, None, a < RA - 1)
    keep_b = (b >= 1, None, b < RB - 1)

    def inner_conv(s, part):
        for f in range(PART * part, PART * part + PART):
            y = dot(wst[s], held[s, f, :, 0:TILE])
            total = None
            for dj in range(3):
                column = None
                for di in range(3):
                    tap = 3 * di + dj
                    term = y[CB * tap : CB * tap + CB]
                    if di != 1:
                        term = pltpu.roll(term, (-(di - 1) * RB) % TILE, 1)
                        term = jnp.where(keep_a[di], term, 0.0)
                    column = term if column is None else column + term
                if dj != 1:
                    column = pltpu.roll(column, (-(dj - 1)) % TILE, 1)
                    column = jnp.where(keep_b[dj], column, 0.0)
                total = column if total is None else total + column
            pre[f] = total

    def ring_conv(s):
        for f in range(FACES):
            y = dot(wst[s], held[s, f, :, TILE:WIDE])
            edge = jnp.concatenate([y[CB * tap : CB * tap + CB] for tap in range(9)], axis=1)
            high = edge.astype(BF16)
            ringy[f, 0:CB, :] = high
            ringy[f, CB : 2 * CB, :] = (edge - high.astype(F32)).astype(BF16)

        def add_ring(g, carry):
            first = pl.multiple_of(4 * g, 4)
            cells = ringy[pl.ds(first, 4)].reshape(8 * CB, 9 * RING)
            extra = dot(cells, sconv[...]).reshape(4, 2, CB, TILE)
            v = pre[pl.ds(first, 4)] + extra[:, 0] + extra[:, 1]
            if s == 0:
                sig = 1.0 / (1.0 + jnp.exp(-v))
                act_ref[pl.ds(first, 4)] = (v * sig).astype(BF16)
                slope = cot_ref[pl.ds(first, 4)].astype(F32) * sig * (1.0 + v * (1.0 - sig))
                held[1, pl.ds(first, 4), rows(ch), 0:TILE] = slope.astype(BF16)
            else:
                grad_ref[pl.ds(first, 4)] = v.astype(BF16)
            return carry

        lax.fori_loop(0, FACES // 4, add_ring, 0)

    for s in range(2):
        if s == 1:
            pack(1)
        for n, (dx, dy, kind, slot) in enumerate(HALO):

            @pl.when(inside(px + dx, py + dy))
            def _():
                halo_copy(s, n).start()

        send_lines(s)
        for index in (Z, XU, XD, Z + 1, Z + 2, Z + 3):
            ag_copy(s, index).start()

        def came(*indices):
            for index in indices:
                ag_copy(s, index).wait_recv()

        def go(*indices):
            for index in indices:
                ag_copy(s, index).start()

        def ring_came(*indices):
            for index in indices:
                rg_copy(s, index).wait_recv()

        def ring_go(*indices):
            for index in indices:
                rg_copy(s, index).start()

        came(XU, XD)
        go(FU, FD)
        came(Z)
        go(ZU, ZD)
        came(Z + 1)
        go(ZU + 1, ZD + 1)
        for n, (dx, dy, kind, slot) in enumerate(HALO):

            @pl.when(inside(px - dx, py - dy))
            def _():
                halo_copy(s, n).wait_recv()

        take_lines(s)
        make_ring(s)
        ring_go(0, 1, 2)
        came(Z + 2)
        go(ZU + 2, ZD + 2)
        came(Z + 3)
        go(ZU + 3, ZD + 3)
        came(ZU)
        go(ZF)
        came(ZU + 1)
        go(ZF + 1)
        ring_came(1, 2)
        ring_go(5, 6)
        ring_came(0)
        ring_go(3, 4)
        came(ZD + 2)
        go(ZF + 2)
        came(ZD + 3)
        go(ZF + 3)
        came(FU, FD, ZD, ZF)
        inner_conv(s, 0)
        ring_came(3, 4)
        ring_go(7, 8)
        came(ZD + 1, ZF + 1)
        inner_conv(s, 1)
        came(ZU + 2, ZF + 2)
        inner_conv(s, 2)
        came(ZU + 3, ZF + 3)
        inner_conv(s, 3)
        ring_came(5, 6, 7, 8)
        ring_conv(s)

    for s in range(2):
        for index in range(ZF + 4):
            ag_copy(s, index).wait_send()
        for index in range(9):
            rg_copy(s, index).wait_send()
        for n, (dx, dy, kind, slot) in enumerate(HALO):

            @pl.when(inside(px + dx, py + dy))
            def _():
                halo_copy(s, n).wait_send()

        for side in range(4):

            @pl.when(sides[side])
            def _():
                many_lines(s, len(BORDER) - 1, line_send.at[s, side], line_recv.at[s]).wait_send()


def local(features, cotangent, weight, edge_table, corner_table):
    def by_face(v):
        return jnp.transpose(v.reshape(CB, FACES, TILE), (1, 0, 2))

    vmem = pl.BlockSpec(memory_space=pltpu.VMEM)
    smem = pl.BlockSpec(memory_space=pltpu.SMEM)
    hbm = pl.BlockSpec(memory_space=pl.ANY)
    field = jax.ShapeDtypeStruct((FACES, CB, TILE), BF16)
    act, grad = pl.pallas_call(
        kernel,
        out_shape=(field, field),
        in_specs=[smem, smem, hbm, hbm, hbm],
        out_specs=(vmem, vmem),
        scratch_shapes=[
            pltpu.VMEM((2, FACES, 8 * CB, WIDE), BF16),
            pltpu.VMEM((FACES, CB, TILE), BF16),
            pltpu.VMEM((9, 8 * CB, 8 * CB), BF16),
            pltpu.VMEM((2, 3, 3 * CB, 128), BF16),
            pltpu.VMEM((2, 8, 3 * CB, 128), BF16),
            pltpu.VMEM((2, SLOTS, 3 * CB, 128), BF16),
            pltpu.VMEM((48, CB, 128), BF16),
            pltpu.VMEM((FACES, CB, RING), F32),
            pltpu.VMEM((FACES, CB, TILE), F32),
            pltpu.VMEM((FACES, 2 * CB, 9 * RING), BF16),
            pltpu.VMEM((2, 9 * CB, 128), BF16),
            pltpu.VMEM((4, TILE, 384), BF16),
            pltpu.VMEM((1024, 512), BF16),
            pltpu.VMEM((4, 128, 256), BF16),
            pltpu.VMEM((4, 128, 256), BF16),
            pltpu.VMEM((9 * RING, TILE), BF16),
            pltpu.SemaphoreType.DMA((3,)),
            pltpu.SemaphoreType.DMA((2, ZF + 4)),
            pltpu.SemaphoreType.DMA((2, ZF + 4)),
            pltpu.SemaphoreType.DMA((2, 9)),
            pltpu.SemaphoreType.DMA((2, 9)),
            pltpu.SemaphoreType.DMA((2, 8)),
            pltpu.SemaphoreType.DMA((2, 8)),
            pltpu.SemaphoreType.DMA((2, 4)),
            pltpu.SemaphoreType.DMA((2,)),
        ],
        compiler_params=pltpu.CompilerParams(
            collective_id=0, has_side_effects=True, vmem_limit_bytes=56 * 1024 * 1024
        ),
        name="conv_pair",
    )(
        jnp.transpose(edge_table, (2, 1, 0)),
        jnp.transpose(corner_table, (1, 2, 0)),
        by_face(features),
        by_face(cotangent),
        weight.reshape(9, 8 * CB, 8 * CB),
    )

    def by_channel(v):
        return jnp.transpose(v, (1, 0, 2)).reshape(CB, FACES, 1, 1, TILE)

    return by_channel(act), by_channel(grad)


def solution(mesh):
    field = P("ch", None, "py", "px", None)
    return jax.shard_map(
        local,
        mesh=mesh,
        in_specs=(field, field, P(), P(), P()),
        out_specs=(field, field),
        check_vma=False,
    )
```

time: 103 us -> 75 us (0.73)
  the two profiles are of different devices: /device:TPU:2 before, /device:TPU:32 now
where the time goes in v2:
time: 75 us; the launch traced here: 74.8 us
  Pallas kernels  71.8 us (96%)
  local copies, waits for them, and re-layouts  2.34 us (3%)
    pallas_call x1, Pallas kernels, local(): pl.pallas_call(kernel, out_shape=(field, field), in_specs=[smem, smem, hb...  71.8 us
    unnamed x4, local copies, waits for them, and re-layouts  2.34 us

profile of v2, /device:TPU:32, one launch (start us, length us, event | category | flops | bytes accessed | tf_op | source)
XLA Modules:
  0.0 74.8 jit_solution(8002332612525174617)
XLA Ops:
  0.6 71.8 %conv_pair.1 = (bf16[12,16,512]{2,1,0:T(8,128)(2,1)}, bf16[12,16,512]{2,1,0:T(8,128)(2,1)}) custom-call(s32[3,4,12]{2,1,0:T(4,128)} %bitcast.24, s32[4,2,12]{2,1,0:T(2,128)} %bitcast.25, bf16[12,16,512]{2,1,0:T(8,128)(2,1)} %bitcast.22, bf16[12,16,512]{2,1,0:T(8,128)(2,1)} %bitcast.23, bf16[9,128,128]{2,1,0:T(8,128)(2,1)} %bitcast.19), custom_call_target="tpu_custom_call" | custom-call | tf_op jit(solution)/shard_map/conv_pair/pallas_call | solution.py:527
  72.5 0.0 copy-start
  72.5 1.7 %copy.11 = bf16[16,12,1,1,512]{4,0,3,2,1:T(8,128)(2,1)} copy(bf16[16,12,1,1,512]{4,0,3,2,1:T(8,128)(2,1)} %bitcast.21) | data formatting | bytes 393216
  74.1 0.0 copy-done
  74.1 0.7 copy.12
Async XLA Ops:
  72.5 1.7 %copy-start = (bf16[12,16,512]{2,1,0:T(8,128)(2,1)S(1)}, bf16[12,16,512]{2,1,0:T(8,128)(2,1)}, u32[]{:S(2)}) copy-start(bf16[12,16,512]{2,1,0:T(8,128)(2,1)} %get-tuple-element.5) | copy-start | bytes 589828

commit v3 on v2

--- a/solution.py
+++ b/solution.py
@@ -34,8 +34,7 @@
     if qx in (0, N_PX - 1) or qy in (0, N_PY - 1)
 )
 SLOTS = 2 * N_PX + 2 * N_PY
-PART = 3
-PARTS = FACES // PART
+PARTS = ((0, 3), (3, 3), (6, 3), (9, 3))
 Z, XU, XD, FU, FD, ZU, ZD, ZF = 0, 4, 5, 6, 7, 8, 12, 16
 
 
@@ -120,9 +119,11 @@
     feat_ref,
     cot_hbm,
     w_hbm,
+    act_hbm,
+    grad_hbm,
+    held,
     act_ref,
     grad_ref,
-    held,
     cot_ref,
     w_ref,
     bd,
@@ -153,6 +154,7 @@
     up_x = z * N_X + (x + 1) % N_X
     down_x = z * N_X + (x + N_X - 1) % N_X
     far = (1 - z) * N_X + x
+    opp_x = z * N_X + (x + 2) % N_X
     far_up = (1 - z) * N_X + (x + 1) % N_X
     far_down = (1 - z) * N_X + (x + N_X - 1) % N_X
     sides = (py == 0, py == N_PY - 1, px == 0, px == N_PX - 1)
@@ -169,6 +171,11 @@
     )
     for load in loads:
         load.start()
+    keep_act = pltpu.make_async_copy(act_ref, act_hbm, load_sem.at[3])
+
+    def keep_grad(g):
+        part = pl.ds(pl.multiple_of(4 * g, 4), 4)
+        return pltpu.make_async_copy(grad_ref.at[part], grad_hbm.at[part], load_sem.at[4 + g])
 
     barrier = pltpu.get_barrier_semaphore()
 
@@ -182,7 +189,7 @@
         return carry
 
     lax.fori_loop(0, N_PX * N_PY, greet, 0)
-    for peer in (far, up_x, down_x):
+    for peer in (far, up_x, down_x, opp_x):
         pl.semaphore_signal(barrier, inc=1, device_id={"ch": peer}, device_id_type=MESH)
 
     def pack(s):
@@ -217,7 +224,7 @@
                 hal[s, slot] = jnp.zeros((3 * CB, 128), BF16)
 
     loads[2].wait()
-    pl.semaphore_wait(barrier, N_PX * N_PY - 1 + 3)
+    pl.semaphore_wait(barrier, N_PX * N_PY - 1 + 4)
 
     def remote(ref, send, recv, device, dst=None):
         return pltpu.make_async_remote_copy(
@@ -231,7 +238,7 @@
 
     def ag_copy(s, index):
         if index < XU:
-            block, target, first, count = ch, far, PART * index, PART
+            block, target, (first, count) = ch, far, PARTS[index]
         elif index < ZU:
             block, target, first, count = (
                 (ch, up_x, 0, FACES),
@@ -241,12 +248,11 @@
             )[index - XU]
         elif index < ZF:
             part = (index - ZU) % 4
-            block, target = far, up_x if index < ZD else down_x
-            first, count = PART * part, PART
+            block, target, (first, count) = far, up_x if index < ZD else down_x, PARTS[part]
         else:
             part = index - ZF
-            block, target = (far_down, up_x) if part < 2 else (far_up, down_x)
-            first, count = PART * part, PART
+            block, target = ((far_down, up_x), (far_up, down_x), (far, opp_x), (far, opp_x))[part]
+            first, count = PARTS[part]
         ref = held.at[s, pl.ds(first, count), rows(block), pl.ds(0, TILE)]
         return remote(ref, ag_send.at[s, index], ag_recv.at[s, index], {"ch": target})
 
@@ -257,10 +263,8 @@
             (ch, down_x, 0, 12),
             (far, up_x, 0, 12),
             (far, down_x, 0, 12),
-            (down_x, up_x, 0, 6),
-            (up_x, down_x, 6, 6),
-            (far_down, up_x, 0, 6),
-            (far_up, down_x, 6, 6),
+            (ch, opp_x, 0, 12),
+            (far, opp_x, 0, 12),
         )[index]
         ref = held.at[s, pl.ds(first, count), rows(block), pl.ds(TILE, RING)]
         return remote(ref, rg_send.at[s, index], rg_recv.at[s, index], {"ch": target})
@@ -383,7 +387,7 @@
     keep_b = (b >= 1, None, b < RB - 1)
 
     def inner_conv(s, part):
-        for f in range(PART * part, PART * part + PART):
+        for f in range(PARTS[part][0], sum(PARTS[part])):
             y = dot(wst[s], held[s, f, :, 0:TILE])
             total = None
             for dj in range(3):
@@ -421,9 +425,12 @@
                 held[1, pl.ds(first, 4), rows(ch), 0:TILE] = slope.astype(BF16)
             else:
                 grad_ref[pl.ds(first, 4)] = v.astype(BF16)
+                keep_grad(g).start()
             return carry
 
         lax.fori_loop(0, FACES // 4, add_ring, 0)
+        if s == 0:
+            keep_act.start()
 
     for s in range(2):
         if s == 1:
@@ -435,8 +442,12 @@
                 halo_copy(s, n).start()
 
         send_lines(s)
-        for index in (Z, XU, XD, Z + 1, Z + 2, Z + 3):
+        for index in (Z, XU, XD):
             ag_copy(s, index).start()
+
+        def sent(*indices):
+            for index in indices:
+                ag_copy(s, index).wait_send()
 
         def came(*indices):
             for index in indices:
@@ -454,10 +465,16 @@
             for index in indices:
                 rg_copy(s, index).start()
 
+        sent(Z)
+        go(Z + 1)
+        sent(Z + 1)
+        go(Z + 2)
         came(XU, XD)
         go(FU, FD)
         came(Z)
         go(ZU, ZD)
+        sent(Z + 2)
+        go(Z + 3)
         came(Z + 1)
         go(ZU + 1, ZD + 1)
         for n, (dx, dy, kind, slot) in enumerate(HALO):
@@ -468,40 +485,32 @@
 
         take_lines(s)
         make_ring(s)
-        ring_go(0, 1, 2)
+        ring_go(0, 1, 2, 5)
         came(Z + 2)
-        go(ZU + 2, ZD + 2)
-        came(Z + 3)
-        go(ZU + 3, ZD + 3)
+        go(ZU + 2, ZD + 2, ZF + 2)
         came(ZU)
         go(ZF)
-        came(ZU + 1)
+        came(ZD + 1)
         go(ZF + 1)
-        ring_came(1, 2)
-        ring_go(5, 6)
+        came(Z + 3)
+        go(ZU + 3, ZD + 3, ZF + 3)
         ring_came(0)
-        ring_go(3, 4)
-        came(ZD + 2)
-        go(ZF + 2)
-        came(ZD + 3)
-        go(ZF + 3)
+        ring_go(3, 4, 6)
         came(FU, FD, ZD, ZF)
         inner_conv(s, 0)
-        ring_came(3, 4)
-        ring_go(7, 8)
-        came(ZD + 1, ZF + 1)
+        came(ZU + 1, ZF + 1)
         inner_conv(s, 1)
-        came(ZU + 2, ZF + 2)
+        came(ZU + 2, ZD + 2, ZF + 2)
         inner_conv(s, 2)
-        came(ZU + 3, ZF + 3)
+        came(ZU + 3, ZD + 3, ZF + 3)
         inner_conv(s, 3)
-        ring_came(5, 6, 7, 8)
+        ring_came(1, 2, 3, 4, 5, 6)
         ring_conv(s)
 
     for s in range(2):
-        for index in range(ZF + 4):
+        for index in range(Z + 3, ZF + 4):
             ag_copy(s, index).wait_send()
-        for index in range(9):
+        for index in range(7):
             rg_copy(s, index).wait_send()
         for n, (dx, dy, kind, slot) in enumerate(HALO):
 
@@ -515,12 +524,15 @@
             def _():
                 many_lines(s, len(BORDER) - 1, line_send.at[s, side], line_recv.at[s]).wait_send()
 
+    keep_act.wait()
+    for g in range(FACES // 4):
+        keep_grad(g).wait()
+
 
 def local(features, cotangent, weight, edge_table, corner_table):
     def by_face(v):
         return jnp.transpose(v.reshape(CB, FACES, TILE), (1, 0, 2))
 
-    vmem = pl.BlockSpec(memory_space=pltpu.VMEM)
     smem = pl.BlockSpec(memory_space=pltpu.SMEM)
     hbm = pl.BlockSpec(memory_space=pl.ANY)
     field = jax.ShapeDtypeStruct((FACES, CB, TILE), BF16)
@@ -528,9 +540,11 @@
         kernel,
         out_shape=(field, field),
         in_specs=[smem, smem, hbm, hbm, hbm],
-        out_specs=(vmem, vmem),
+        out_specs=(hbm, hbm),
         scratch_shapes=[
             pltpu.VMEM((2, FACES, 8 * CB, WIDE), BF16),
+            pltpu.VMEM((FACES, CB, TILE), BF16),
+            pltpu.VMEM((FACES, CB, TILE), BF16),
             pltpu.VMEM((FACES, CB, TILE), BF16),
             pltpu.VMEM((9, 8 * CB, 8 * CB), BF16),
             pltpu.VMEM((2, 3, 3 * CB, 128), BF16),
@@ -546,7 +560,7 @@
             pltpu.VMEM((4, 128, 256), BF16),
             pltpu.VMEM((4, 128, 256), BF16),
             pltpu.VMEM((9 * RING, TILE), BF16),
-            pltpu.SemaphoreType.DMA((3,)),
+            pltpu.SemaphoreType.DMA((7,)),
             pltpu.SemaphoreType.DMA((2, ZF + 4)),
             pltpu.SemaphoreType.DMA((2, ZF + 4)),
             pltpu.SemaphoreType.DMA((2, 9)),

time: 75 us -> 72.4 us (0.965)
  the two profiles are of different devices: /device:TPU:32 before, /device:TPU:56 now
where the time goes in v3:
time: 72.4 us; the launch traced here: 72.2 us
  Pallas kernels  69.3 us (96%)
  local copies, waits for them, and re-layouts  2.34 us (3%)
    pallas_call x1, Pallas kernels, local(): pl.pallas_call(kernel, out_shape=(field, field), in_specs=[smem, smem, hb...  69.3 us
    unnamed x4, local copies, waits for them, and re-layouts  2.34 us

profile of v3, /device:TPU:56, one launch (start us, length us, event | category | flops | bytes accessed | tf_op | source)
XLA Modules:
  0.0 72.2 jit_solution(2634856346284915166)
XLA Ops:
  0.6 69.3 %conv_pair.1 = (bf16[12,16,512]{2,1,0:T(8,128)(2,1)}, bf16[12,16,512]{2,1,0:T(8,128)(2,1)}) custom-call(s32[3,4,12]{2,1,0:T(4,128)} %bitcast.24, s32[4,2,12]{2,1,0:T(2,128)} %bitcast.25, bf16[12,16,512]{2,1,0:T(8,128)(2,1)} %bitcast.22, bf16[12,16,512]{2,1,0:T(8,128)(2,1)} %bitcast.23, bf16[9,128,128]{2,1,0:T(8,128)(2,1)} %bitcast.19), custom_call_target="tpu_custom_call" | custom-call | tf_op jit(solution)/shard_map/conv_pair/pallas_call | solution.py:539
  69.9 0.0 copy-start
  69.9 1.7 %copy.11 = bf16[16,12,1,1,512]{4,0,3,2,1:T(8,128)(2,1)} copy(bf16[16,12,1,1,512]{4,0,3,2,1:T(8,128)(2,1)} %bitcast.21) | data formatting | bytes 393216
  71.6 0.0 copy-done
  71.6 0.7 copy.12
Async XLA Ops:
  69.9 1.7 %copy-start = (bf16[12,16,512]{2,1,0:T(8,128)(2,1)S(1)}, bf16[12,16,512]{2,1,0:T(8,128)(2,1)}, u32[]{:S(2)}) copy-start(bf16[12,16,512]{2,1,0:T(8,128)(2,1)} %get-tuple-element.5) | copy-start | bytes 589828

commit v4 on v3

--- a/solution.py
+++ b/solution.py
@@ -27,13 +27,8 @@
     (1, -1, 0, 6),
     (-1, -1, 0, 7),
 )
-BORDER = tuple(
-    (qx, qy)
-    for qx in range(N_PX)
-    for qy in range(N_PY)
-    if qx in (0, N_PX - 1) or qy in (0, N_PY - 1)
-)
-SLOTS = 2 * N_PX + 2 * N_PY
+LONE = ((1, 0), (2, 0), (1, N_PY - 1), (2, N_PY - 1))
+FANOUT = 2 * (N_PY // 2) + len(LONE) - 1
 PARTS = ((0, 3), (3, 3), (6, 3), (9, 3))
 Z, XU, XD, FU, FD, ZU, ZD, ZF = 0, 4, 5, 6, 7, 8, 12, 16
 
@@ -50,17 +45,12 @@
     return jnp.dot(a, b, preferred_element_type=F32)
 
 
-def fill_packers(px, py, sbd):
+def fill_packers(py, sbd):
     p, n = iota((TILE, 128), 0), iota((TILE, 128), 1)
-    i, j = n % 32, (n // 32 - px) & 3
-    for kind in range(2):
-        hit = p == (RA - 1) * RB * kind + i
-        for k in range(4):
-            sbd[k, :, 128 * kind : 128 * kind + 128] = ones_where(hit & (j == k))
     i, m = n % 16, (n // 16 - py) & 7
     hit = p == RB * i + jnp.where(m >= 4, RB - 1, 0)
     for k in range(4):
-        sbd[k, :, 256:384] = ones_where(hit & ((m & 3) == k))
+        sbd[k] = ones_where(hit & ((m & 3) == k))
 
 
 def fill_selectors(px, py, sring, sedge, scorner, sconv):
@@ -127,12 +117,15 @@
     cot_ref,
     w_ref,
     bd,
+    bdc,
     hal,
-    lin,
+    linr,
+    linc,
     full,
     ring,
     pre,
     ringy,
+    extra,
     wst,
     sbd,
     sring,
@@ -148,6 +141,8 @@
     halo_recv,
     line_send,
     line_recv,
+    pair_send,
+    pair_recv,
 ):
     px, py, ch = lax.axis_index("px"), lax.axis_index("py"), lax.axis_index("ch")
     z, x = ch // N_X, ch % N_X
@@ -159,7 +154,8 @@
     far_down = (1 - z) * N_X + (x + N_X - 1) % N_X
     sides = (py == 0, py == N_PY - 1, px == 0, px == N_PX - 1)
     border = sides[0] | sides[1] | sides[2] | sides[3]
-    at_corner = (sides[0] | sides[1]) & (sides[2] | sides[3])
+    at_row, at_col = sides[0] | sides[1], sides[2] | sides[3]
+    odd = py % 2
 
     def rows(c):
         return pl.ds(pl.multiple_of(CB * c, CB), CB)
@@ -192,6 +188,19 @@
     for peer in (far, up_x, down_x, opp_x):
         pl.semaphore_signal(barrier, inc=1, device_id={"ch": peer}, device_id_type=MESH)
 
+    def pack_rows(s, lanes, turn):
+        lane = iota((3 * CB, 128), 1)
+        packed = None
+        for k in range(4):
+            part = jnp.concatenate(
+                [held[s, 4 * q + k, rows(ch), lanes : lanes + 128] for q in range(3)], axis=0
+            ).astype(F32)
+            shift = (32 * (k + turn)) % 128
+            if shift:
+                part = pltpu.roll(part, shift, 1)
+            packed = part if packed is None else jnp.where(lane // 32 == k, part, packed)
+        return pltpu.roll(packed, 32 * px, 1).astype(BF16)
+
     def pack(s):
         packed = None
         for k in range(4):
@@ -200,11 +209,16 @@
             )
             term = dot(part, sbd[k])
             packed = term if packed is None else packed + term
-        packed = packed.astype(BF16)
-        for kind in range(3):
-            bd[s, kind] = packed[:, 128 * kind : 128 * kind + 128]
-
-    fill_packers(px, py, sbd)
+        cols = packed
+        bd[s, 0] = pack_rows(s, 0, 0)
+        bd[s, 1] = pack_rows(s, TILE - 128, 1)
+        bd[s, 2] = cols.astype(BF16)
+        first = (((iota((CB, 128), 1) // 16 - py) & 7) < 4) == (px == 0)
+        folded = jnp.where(first, cols[0:CB], pltpu.roll(cols[CB : 2 * CB], 64, 1))
+        bdc[s, 0:CB, :] = folded.astype(BF16)
+        bdc[s, CB : 2 * CB, :] = cols[2 * CB : 3 * CB].astype(BF16)
+
+    fill_packers(py, sbd)
     loads[0].wait()
     pack(0)
     fill_selectors(px, py, sring, sedge, scorner, sconv)
@@ -282,39 +296,86 @@
     def inside(qx, qy):
         return (qx >= 0) & (qx < N_PX) & (qy >= 0) & (qy < N_PY)
 
-    my_slots = (px, N_PX + px, 2 * N_PX + py, 2 * N_PX + N_PY + py)
-
-    def many_lines(s, count, send, recv):
-        ref = lin.at[s, pl.ds(0, count)]
-        return remote(ref, send, recv, {"px": px, "py": py})
+    row_kind = py // (N_PY - 1)
+    row_slot = N_PX * row_kind + px
+    col_slot = N_PY * odd + (N_PY // 2) * (px // (N_PX - 1)) + py // 2
+    here = {"px": px, "py": py}
+
+    def line_copy(s, cols, device):
+        if cols:
+            return remote(
+                bdc.at[s],
+                line_send.at[s, 1],
+                line_recv.at[s, 1],
+                device,
+                linc.at[s, col_slot],
+            )
+        return remote(
+            bd.at[s, row_kind],
+            line_send.at[s, 0],
+            line_recv.at[s, 0],
+            device,
+            linr.at[s, row_slot],
+        )
+
+    def many_lines(s, cols, count):
+        ref = (linc if cols else linr).at[s, pl.ds(0, count)]
+        return remote(ref, line_send.at[s, cols], line_recv.at[s, cols], here)
+
+    def pair_copy(s, cols):
+        if cols:
+            ref = linc.at[s, pl.ds(pl.multiple_of(N_PY * odd, N_PY), N_PY)]
+        else:
+            ref = linr.at[s, pl.ds(pl.multiple_of(N_PX * odd, N_PX), N_PX)]
+        return remote(
+            ref, pair_send.at[s, cols], pair_recv.at[s, cols], {"py": py + 1 - 2 * odd}
+        )
 
     def send_lines(s):
-        for side in range(4):
-
-            @pl.when(sides[side])
-            def _():
-                for tx, ty in BORDER:
+        for cols in range(2):
+
+            @pl.when((at_row, at_col)[cols])
+            def _():
+                for tx in (0, N_PX - 1):
+                    for j in range(N_PY // 2):
+                        ty = 2 * j + odd
+
+                        @pl.when((px != tx) | (py != ty))
+                        def _():
+                            line_copy(s, cols, {"px": tx, "py": ty}).start()
+
+                for tx, ty in LONE:
 
                     @pl.when((px != tx) | (py != ty))
                     def _():
-                        remote(
-                            bd.at[s, min(side, 2)],
-                            line_send.at[s, side],
-                            line_recv.at[s],
-                            {"px": tx, "py": ty},
-                            lin.at[s, my_slots[side]],
-                        ).start()
-
-                lin[s, my_slots[side]] = bd[s, min(side, 2)]
+                        line_copy(s, cols, {"px": tx, "py": ty}).start()
+
+                if cols:
+                    linc[s, col_slot] = bdc[s]
+                else:
+                    linr[s, row_slot] = bd[s, row_kind]
 
     def take_lines(s):
-        @pl.when(at_corner)
+        @pl.when(at_col)
         def _():
-            many_lines(s, SLOTS - 2, line_send.at[s, 0], line_recv.at[s]).wait_recv()
-
-        @pl.when(border & jnp.logical_not(at_corner))
+            @pl.when(at_row)
+            def _():
+                many_lines(s, 0, N_PX - 1).wait_recv()
+
+            @pl.when(jnp.logical_not(at_row))
+            def _():
+                many_lines(s, 0, N_PX).wait_recv()
+
+            pair_copy(s, 0).start()
+            many_lines(s, 1, N_PY - 1).wait_recv()
+            pair_copy(s, 1).start()
+            for cols in range(2):
+                pair_copy(s, cols).wait_recv()
+
+        @pl.when(at_row & jnp.logical_not(at_col))
         def _():
-            many_lines(s, SLOTS - 1, line_send.at[s, 0], line_recv.at[s]).wait_recv()
+            many_lines(s, 0, 2 * N_PX - 1).wait_recv()
+            many_lines(s, 1, 2 * N_PY).wait_recv()
 
     def make_ring(s):
         cells = jnp.concatenate([hal[s, slot] for slot in range(8)], axis=1)
@@ -326,26 +387,34 @@
         @pl.when(border)
         def _():
             lane = iota((3 * CB, 128), 1)
-            for side in range(4):
-                first, count, width, item = (
-                    (0, N_PX, 32, 0),
-                    (N_PX, N_PX, 32, 0),
-                    (2 * N_PX, N_PY, 16, 0),
-                    (2 * N_PX + N_PY, N_PY, 16, 4),
-                )[side]
-                parts = [lin[s, first + q].astype(F32) for q in range(count)]
+            for side in range(2):
+                parts = [linr[s, N_PX * side + j].astype(F32) for j in range(N_PX)]
                 for k in range(4):
                     line = parts[0]
-                    for q in range(1, count):
-                        line = jnp.where(
-                            lane // width == (item + k + q) % count, parts[q], line
-                        )
-                    turn = (-width * (item + k)) % 128
-                    if turn:
-                        line = pltpu.roll(line, turn, 1)
+                    for j in range(1, N_PX):
+                        line = jnp.where(lane // 32 == (k + j) % 4, parts[j], line)
+                    if k:
+                        line = pltpu.roll(line, 128 - 32 * k, 1)
                     line = line.astype(BF16)
                     for q in range(3):
                         full[12 * side + 4 * q + k] = line[CB * q : CB * q + CB, :]
+            lane = iota((2 * CB, 128), 1)
+            for last in range(2):
+                parts = [
+                    linc[s, N_PY * (j % 2) + (N_PY // 2) * last + j // 2].astype(F32)
+                    for j in range(N_PY)
+                ]
+                for m in range(8):
+                    line = parts[0]
+                    for j in range(1, N_PY):
+                        line = jnp.where(lane // 16 == (m + j) % 8, parts[j], line)
+                    if m:
+                        line = pltpu.roll(line, 128 - 16 * m, 1)
+                    line = line.astype(BF16)
+                    face = (m + 4 * last) % 8
+                    full[12 * (2 + last) + face] = line[0:CB, :]
+                    if face < 4:
+                        full[12 * (2 + last) + 8 + face] = line[CB : 2 * CB, :]
             for edge in range(4):
 
                 @pl.when(sides[edge])
@@ -413,11 +482,13 @@
             ringy[f, 0:CB, :] = high
             ringy[f, CB : 2 * CB, :] = (edge - high.astype(F32)).astype(BF16)
 
+        cells = ringy[...].reshape(2 * CB * FACES, 9 * RING)
+        extra[...] = dot(cells, sconv[...]).reshape(FACES, 2, CB, TILE)
+
         def add_ring(g, carry):
             first = pl.multiple_of(4 * g, 4)
-            cells = ringy[pl.ds(first, 4)].reshape(8 * CB, 9 * RING)
-            extra = dot(cells, sconv[...]).reshape(4, 2, CB, TILE)
-            v = pre[pl.ds(first, 4)] + extra[:, 0] + extra[:, 1]
+            more = extra[pl.ds(first, 4)]
+            v = pre[pl.ds(first, 4)] + more[:, 0] + more[:, 1]
             if s == 0:
                 sig = 1.0 / (1.0 + jnp.exp(-v))
                 act_ref[pl.ds(first, 4)] = (v * sig).astype(BF16)
@@ -442,7 +513,7 @@
                 halo_copy(s, n).start()
 
         send_lines(s)
-        for index in (Z, XU, XD):
+        for index in (Z, XU, XD, Z + 1, Z + 2, Z + 3):
             ag_copy(s, index).start()
 
         def sent(*indices):
@@ -465,16 +536,10 @@
             for index in indices:
                 rg_copy(s, index).start()
 
-        sent(Z)
-        go(Z + 1)
-        sent(Z + 1)
-        go(Z + 2)
         came(XU, XD)
         go(FU, FD)
         came(Z)
         go(ZU, ZD)
-        sent(Z + 2)
-        go(Z + 3)
         came(Z + 1)
         go(ZU + 1, ZD + 1)
         for n, (dx, dy, kind, slot) in enumerate(HALO):
@@ -508,7 +573,7 @@
         ring_conv(s)
 
     for s in range(2):
-        for index in range(Z + 3, ZF + 4):
+        for index in range(Z, ZF + 4):
             ag_copy(s, index).wait_send()
         for index in range(7):
             rg_copy(s, index).wait_send()
@@ -518,11 +583,15 @@
             def _():
                 halo_copy(s, n).wait_send()
 
-        for side in range(4):
-
-            @pl.when(sides[side])
-            def _():
-                many_lines(s, len(BORDER) - 1, line_send.at[s, side], line_recv.at[s]).wait_send()
+        for cols in range(2):
+
+            @pl.when((at_row, at_col)[cols])
+            def _():
+                many_lines(s, cols, FANOUT).wait_send()
+
+            @pl.when(at_col)
+            def _():
+                pair_copy(s, cols).wait_send()
 
     keep_act.wait()
     for g in range(FACES // 4):
@@ -548,14 +617,17 @@
             pltpu.VMEM((FACES, CB, TILE), BF16),
             pltpu.VMEM((9, 8 * CB, 8 * CB), BF16),
             pltpu.VMEM((2, 3, 3 * CB, 128), BF16),
+            pltpu.VMEM((2, 2 * CB, 128), BF16),
             pltpu.VMEM((2, 8, 3 * CB, 128), BF16),
-            pltpu.VMEM((2, SLOTS, 3 * CB, 128), BF16),
+            pltpu.VMEM((2, FANOUT, 3 * CB, 128), BF16),
+            pltpu.VMEM((2, 2 * N_PY, 2 * CB, 128), BF16),
             pltpu.VMEM((48, CB, 128), BF16),
             pltpu.VMEM((FACES, CB, RING), F32),
             pltpu.VMEM((FACES, CB, TILE), F32),
             pltpu.VMEM((FACES, 2 * CB, 9 * RING), BF16),
+            pltpu.VMEM((FACES, 2, CB, TILE), F32),
             pltpu.VMEM((2, 9 * CB, 128), BF16),
-            pltpu.VMEM((4, TILE, 384), BF16),
+            pltpu.VMEM((4, TILE, 128), BF16),
             pltpu.VMEM((1024, 512), BF16),
             pltpu.VMEM((4, 128, 256), BF16),
             pltpu.VMEM((4, 128, 256), BF16),
@@ -567,8 +639,10 @@
             pltpu.SemaphoreType.DMA((2, 9)),
             pltpu.SemaphoreType.DMA((2, 8)),
             pltpu.SemaphoreType.DMA((2, 8)),
-            pltpu.SemaphoreType.DMA((2, 4)),
-            pltpu.SemaphoreType.DMA((2,)),
+            pltpu.SemaphoreType.DMA((2, 2)),
+            pltpu.SemaphoreType.DMA((2, 2)),
+            pltpu.SemaphoreType.DMA((2, 2)),
+            pltpu.SemaphoreType.DMA((2, 2)),
         ],
         compiler_params=pltpu.CompilerParams(
             collective_id=0, has_side_effects=True, vmem_limit_bytes=56 * 1024 * 1024

time: 72.4 us -> 69.7 us (0.963)
  the two profiles are of different devices: /device:TPU:56 before, /device:TPU:1 now
where the time goes in v4:
time: 69.7 us; the launch traced here: 69.5 us
  Pallas kernels  66.5 us (95%)
  local copies, waits for them, and re-layouts  2.34 us (3%)
    pallas_call x1, Pallas kernels, local(): pl.pallas_call(kernel, out_shape=(field, field), in_specs=[smem, smem, hb...  66.5 us
    unnamed x4, local copies, waits for them, and re-layouts  2.34 us

profile of v4, /device:TPU:1, one launch (start us, length us, event | category | flops | bytes accessed | tf_op | source)
XLA Modules:
  0.0 69.5 jit_solution(6910361649062781914)
XLA Ops:
  0.6 66.5 %conv_pair.1 = (bf16[12,16,512]{2,1,0:T(8,128)(2,1)}, bf16[12,16,512]{2,1,0:T(8,128)(2,1)}) custom-call(s32[3,4,12]{2,1,0:T(4,128)} %bitcast.24, s32[4,2,12]{2,1,0:T(2,128)} %bitcast.25, bf16[12,16,512]{2,1,0:T(8,128)(2,1)} %bitcast.22, bf16[12,16,512]{2,1,0:T(8,128)(2,1)} %bitcast.23, bf16[9,128,128]{2,1,0:T(8,128)(2,1)} %bitcast.19), custom_call_target="tpu_custom_call" | custom-call | tf_op jit(solution)/shard_map/conv_pair/pallas_call | solution.py:608
  67.1 0.0 copy-start
  67.2 1.7 %copy.11 = bf16[16,12,1,1,512]{4,0,3,2,1:T(8,128)(2,1)} copy(bf16[16,12,1,1,512]{4,0,3,2,1:T(8,128)(2,1)} %bitcast.21) | data formatting | bytes 393216
  68.8 0.0 copy-done
  68.8 0.7 copy.12
Async XLA Ops:
  67.1 1.7 %copy-start = (bf16[12,16,512]{2,1,0:T(8,128)(2,1)S(1)}, bf16[12,16,512]{2,1,0:T(8,128)(2,1)}, u32[]{:S(2)}) copy-start(bf16[12,16,512]{2,1,0:T(8,128)(2,1)} %get-tuple-element.5) | copy-start | bytes 589828

commit v5 on v4

--- a/solution.py
+++ b/solution.py
@@ -109,11 +109,9 @@
     feat_ref,
     cot_hbm,
     w_hbm,
-    act_hbm,
-    grad_hbm,
-    held,
     act_ref,
     grad_ref,
+    held,
     cot_ref,
     w_ref,
     bd,
@@ -167,12 +165,6 @@
     )
     for load in loads:
         load.start()
-    keep_act = pltpu.make_async_copy(act_ref, act_hbm, load_sem.at[3])
-
-    def keep_grad(g):
-        part = pl.ds(pl.multiple_of(4 * g, 4), 4)
-        return pltpu.make_async_copy(grad_ref.at[part], grad_hbm.at[part], load_sem.at[4 + g])
-
     barrier = pltpu.get_barrier_semaphore()
 
     def greet(t, carry):
@@ -496,12 +488,9 @@
                 held[1, pl.ds(first, 4), rows(ch), 0:TILE] = slope.astype(BF16)
             else:
                 grad_ref[pl.ds(first, 4)] = v.astype(BF16)
-                keep_grad(g).start()
             return carry
 
         lax.fori_loop(0, FACES // 4, add_ring, 0)
-        if s == 0:
-            keep_act.start()
 
     for s in range(2):
         if s == 1:
@@ -593,10 +582,6 @@
             def _():
                 pair_copy(s, cols).wait_send()
 
-    keep_act.wait()
-    for g in range(FACES // 4):
-        keep_grad(g).wait()
-
 
 def local(features, cotangent, weight, edge_table, corner_table):
     def by_face(v):
@@ -604,16 +589,15 @@
 
     smem = pl.BlockSpec(memory_space=pltpu.SMEM)
     hbm = pl.BlockSpec(memory_space=pl.ANY)
-    field = jax.ShapeDtypeStruct((FACES, CB, TILE), BF16)
+    field = pltpu.VMEM((FACES, CB, TILE), BF16)
+    vmem = pl.BlockSpec(memory_space=pltpu.VMEM)
     act, grad = pl.pallas_call(
         kernel,
         out_shape=(field, field),
         in_specs=[smem, smem, hbm, hbm, hbm],
-        out_specs=(hbm, hbm),
+        out_specs=(vmem, vmem),
         scratch_shapes=[
             pltpu.VMEM((2, FACES, 8 * CB, WIDE), BF16),
-            pltpu.VMEM((FACES, CB, TILE), BF16),
-            pltpu.VMEM((FACES, CB, TILE), BF16),
             pltpu.VMEM((FACES, CB, TILE), BF16),
             pltpu.VMEM((9, 8 * CB, 8 * CB), BF16),
             pltpu.VMEM((2, 3, 3 * CB, 128), BF16),
@@ -632,7 +616,7 @@
             pltpu.VMEM((4, 128, 256), BF16),
             pltpu.VMEM((4, 128, 256), BF16),
             pltpu.VMEM((9 * RING, TILE), BF16),
-            pltpu.SemaphoreType.DMA((7,)),
+            pltpu.SemaphoreType.DMA((3,)),
             pltpu.SemaphoreType.DMA((2, ZF + 4)),
             pltpu.SemaphoreType.DMA((2, ZF + 4)),
             pltpu.SemaphoreType.DMA((2, 9)),

time: 69.7 us -> 68.1 us (0.977)
  local copies, waits for them, and re-layouts: 2.34 us -> 1.36 us
    unnamed x4 -> x2, local copies, waits for them, and re-layouts: 2.34 us -> 1.36 us
where the time goes in v5:
time: 68.1 us; the launch traced here: 68 us
  Pallas kernels  66 us (97%)
  local copies, waits for them, and re-layouts  1.36 us (2%)
    pallas_call x1, Pallas kernels, local(): pl.pallas_call(kernel, out_shape=(field, field), in_specs=[smem, smem, hb...  66 us

profile of v5, /device:TPU:1, one launch (start us, length us, event | category | flops | bytes accessed | tf_op | source)
XLA Modules:
  0.0 68.0 jit_solution(14665436104328149916)
XLA Ops:
  0.6 66.0 %conv_pair.1 = (bf16[12,16,512]{2,1,0:T(8,128)(2,1)S(1)}, bf16[12,16,512]{2,1,0:T(8,128)(2,1)S(1)}) custom-call(s32[3,4,12]{2,1,0:T(4,128)} %bitcast.24, s32[4,2,12]{2,1,0:T(2,128)} %bitcast.25, bf16[12,16,512]{2,1,0:T(8,128)(2,1)} %bitcast.22, bf16[12,16,512]{2,1,0:T(8,128)(2,1)} %bitcast.23, bf16[9,128,128]{2,1,0:T(8,128)(2,1)} %bitcast.21), custom_call_target="tpu_custom_call" | custom-call | tf_op jit(solution)/shard_map/conv_pair/pallas_call | solution.py:594
  66.6 0.7 copy.11
  67.3 0.7 copy.12

commit v6 on v5

--- a/solution.py
+++ b/solution.py
@@ -376,6 +376,8 @@
             for k in range(4):
                 ring[4 * q + k] = inner[CB * q : CB * q + CB, 128 * k : 128 * k + 128]
 
+        take_lines(s)
+
         @pl.when(border)
         def _():
             lane = iota((3 * CB, 128), 1)
@@ -495,13 +497,13 @@
     for s in range(2):
         if s == 1:
             pack(1)
+        send_lines(s)
         for n, (dx, dy, kind, slot) in enumerate(HALO):
 
             @pl.when(inside(px + dx, py + dy))
             def _():
                 halo_copy(s, n).start()
 
-        send_lines(s)
         for index in (Z, XU, XD, Z + 1, Z + 2, Z + 3):
             ag_copy(s, index).start()
 
@@ -537,7 +539,6 @@
             def _():
                 halo_copy(s, n).wait_recv()
 
-        take_lines(s)
         make_ring(s)
         ring_go(0, 1, 2, 5)
         came(Z + 2)

time: 68.1 us -> 67.5 us (level)
  Pallas kernels: 66 us -> 65.3 us
where the time goes in v6:
time: 67.5 us; the launch traced here: 67.3 us
  Pallas kernels  65.3 us (97%)
  local copies, waits for them, and re-layouts  1.36 us (2%)
    pallas_call x1, Pallas kernels, local(): pl.pallas_call(kernel, out_shape=(field, field), in_specs=[smem, smem, hb...  65.3 us
    unnamed x2, local copies, waits for them, and re-layouts  1.36 us

profile of v6, /device:TPU:1, one launch (start us, length us, event | category | flops | bytes accessed | tf_op | source)
XLA Modules:
  0.0 67.3 jit_solution(5022908969727542825)
XLA Ops:
  0.6 65.3 %conv_pair.1 = (bf16[12,16,512]{2,1,0:T(8,128)(2,1)S(1)}, bf16[12,16,512]{2,1,0:T(8,128)(2,1)S(1)}) custom-call(s32[3,4,12]{2,1,0:T(4,128)} %bitcast.24, s32[4,2,12]{2,1,0:T(2,128)} %bitcast.25, bf16[12,16,512]{2,1,0:T(8,128)(2,1)} %bitcast.22, bf16[12,16,512]{2,1,0:T(8,128)(2,1)} %bitcast.23, bf16[9,128,128]{2,1,0:T(8,128)(2,1)} %bitcast.21), custom_call_target="tpu_custom_call" | custom-call | tf_op jit(solution)/shard_map/conv_pair/pallas_call | solution.py:595
  66.0 0.7 %copy.11 = bf16[16,12,1,1,512]{4,0,3,2,1:T(8,128)(2,1)} copy(bf16[16,12,1,1,512]{4,0,3,2,1:T(8,128)(2,1)S(1)} %bitcast.20) | data formatting | bytes 393216
  66.7 0.7 %copy.12 = bf16[16,12,1,1,512]{4,0,3,2,1:T(8,128)(2,1)} copy(bf16[16,12,1,1,512]{4,0,3,2,1:T(8,128)(2,1)S(1)} %bitcast.19) | data formatting | bytes 393216
